TPU v7x, 32 devices: a whole 2x2x4 slice. The times are simulated.
32 devices in a mesh: dp: 16 (over z, y, x), fsdp: 2 (over core).
Axes of the slice: x: 2, y: 2, z: 4, core: 2. Of those that a mesh axis runs over, the one named last changes fastest.
Arguments:
- features: bfloat16 [64, 1128, 512], P(('dp', 'fsdp')), may hold values from -6 to 6
- cotangent: bfloat16 [64, 1128, 512], P(('dp', 'fsdp')), may hold values from -6 to 6
- counts: int32 [64], P(('dp', 'fsdp')), may hold values from 1 to 100, as said below
- weights: float32 [4096, 512], P(('dp', 'fsdp'))
- small_params: float32 [3584], replicated
- moments_old: float32 [2, 4096, 512], P(None, ('dp', 'fsdp')), as said below
- small_moments: float32 [2, 3584], replicated, as said below
- basis_attn: float32 [4, 512, 512], replicated, as said below
- basis_ffn: float32 [2, 1024, 1024], replicated, as said below
- basis_cols: float32 [6, 512, 512], replicated, as said below
Outputs:
- output: bfloat16 [64, 1128, 512], P(('dp', 'fsdp'))
- grad_input: float32 [64, 1128, 512], P(('dp', 'fsdp'))
- grad_weights: float32 [4096, 512], P(('dp', 'fsdp'))
- moments_new: float32 [2, 4096, 512], P(None, ('dp', 'fsdp'))
- weights_new: float32 [4096, 512], P(('dp', 'fsdp'))
- grad_small: float32 [3584], replicated
- small_moments_new: float32 [2, 3584], replicated
- small_new: float32 [3584], replicated
Inputs may be any that keep to these rules, and one draw needn't show every extreme that they name: `counts`: some neighbourhood has 100 live queries and some has 1. `basis_attn`: each of the four matrices is orthogonal. `basis_ffn`: each of the two matrices is orthogonal. `basis_cols`: each of the six matrices is orthogonal. `moments_old`: second moments (index 1) are positive. `small_moments`: second moments (index 1) are positive.
All inputs are finite; a program needn't handle non-finite values.
Results may differ from a plain program's by a relative error of at most 0.014.
The roundings to bfloat16 on the way count: a program that leaves them out, or rounds other values in their place, can miss the bound.
Values may be sent and summed in bfloat16 or wider, within the bound.
No kernel may reach another device: no remote copies, remote signals or barrier semaphores. Data moves between devices by JAX's collectives and lax.ppermute only.
A program may use at most 320 MiB of HBM per device.

v0:
```python
import functools
import jax
import jax.numpy as jnp
from jax import lax
from jax.sharding import PartitionSpec as P
from jax.experimental import pallas as pl
from jax.experimental.pallas import tpu as pltpu

D = 512
HEADS = 4
FF = 1024
HD = 128
CTX = 1024
SLOTS = 1128
STEP = 10
PAD = 1152
RB = 384
NRB = PAD // RB
RBL = 576
SUB = 128
NRBL = PAD // RBL
scaling = HD ** (-0.5)
eps_norm = 1e-05
eps_adam = 1e-08
beta_one = 0.9
beta_two = 0.999
rate_mats = 0.1
rate_small = 0.5
axes = ("dp", "fsdp")
bf16 = jnp.bfloat16
f32 = jnp.float32
VLIM_FWD = 58 * 1024 * 1024
VLIM_ROWS = 46 * 1024 * 1024
VLIM_BWD = 46 * 1024 * 1024
VLIM_STEP = 24 * 1024 * 1024


def nt(a, b):
    return lax.dot_general(a, b, (((1,), (1,)), ((), ())), preferred_element_type=f32)


def nn(a, b):
    return lax.dot_general(a, b, (((1,), (0,)), ((), ())), preferred_element_type=f32)


def tn(a, b):
    return lax.dot_general(a, b, (((0,), (0,)), ((), ())), preferred_element_type=f32)


def put_in_order(me, parts, out):
    def move(j, carry):
        for c, part in enumerate(parts):
            out[(j * len(parts) + c) ^ me] = part[j]
        return carry

    lax.fori_loop(0, parts[0].shape[0], move, 0)


def attn_fwd_body(ways, *refs):
    me_ref, xc_ref, xr_ref, *refs = refs
    parts, (q_ref, k_ref, v_ref, e_ref, o_ref, li_ref, w_ref, ve_ref) = refs[:ways], refs[ways:]
    n, rb = pl.program_id(0), pl.program_id(1)

    @pl.when(jnp.logical_and(n == 0, rb == 0))
    def _():
        put_in_order(me_ref[0] & (w_ref.shape[0] - 1), parts, w_ref)

    @pl.when(rb == 0)
    def _():
        xc = xc_ref[0]
        k_ref[0] = nt(xc, w_ref[:, 1].reshape(D, D)).astype(bf16)
        v_ref[0] = nt(xc, w_ref[:, 2].reshape(D, D)).astype(bf16)
        for h in range(HEADS):
            ve_ref[h, :, 0:HD] = v_ref[0, :, h * HD : (h + 1) * HD]
            ve_ref[h, :, HD : 2 * HD] = jnp.ones((CTX, HD), bf16)

    rows = rb * RB + lax.broadcasted_iota(jnp.int32, (RB, 1), 0)
    xr = jnp.where(rows < SLOTS, xr_ref[0].astype(f32), 0.0).astype(bf16)
    q_ref[0] = (nt(xr, w_ref[:, 0].reshape(D, D)) * scaling).astype(bf16)
    lane = lax.broadcasted_iota(jnp.int32, (SUB, HD), 1) // (HD // HEADS)
    for r in range(0, RB, SUB):
        rs = slice(r, r + SUB)
        for h in range(HEADS):
            hs = slice(h * HD, (h + 1) * HD)
            s = nt(q_ref[0, rs, hs], k_ref[0, :, hs])
            m = jnp.max(s, axis=-1, keepdims=True)
            e = jnp.exp(s - m).astype(bf16)
            e_ref[0, h, rs] = e
            ov = nn(e, ve_ref[h])
            li = 1.0 / ov[:, HD:]
            scales = li if h == 0 else jnp.where(lane == h, li, scales)
            o_ref[0, rs, hs] = (ov[:, :HD] * li).astype(bf16)
        li_ref[0, rs] = scales


def attn_fwd(x, parts, me):
    n = x.shape[0]
    sd = jax.ShapeDtypeStruct
    everything = lambda shape: pl.BlockSpec(shape, lambda i, r: (0,) * len(shape))
    wshape = (len(parts) * parts[0].shape[0],) + parts[0].shape[1:]
    block = lambda w: pl.BlockSpec((1, RB, w), lambda i, r: (i, r, 0))
    context = pl.BlockSpec((1, CTX, D), lambda i, r: (i, 0, 0))
    return pl.pallas_call(
        functools.partial(attn_fwd_body, len(parts)),
        grid=(n, NRB),
        in_specs=[pl.BlockSpec(memory_space=pltpu.SMEM), context, block(D)]
        + [everything(w.shape) for w in parts],
        out_specs=[
            block(D),
            context,
            context,
            pl.BlockSpec((1, HEADS, RB, CTX), lambda i, r: (i, 0, r, 0)),
            block(D),
            block(HD),
            everything(wshape),
        ],
        out_shape=[
            sd((n, PAD, D), bf16),
            sd((n, CTX, D), bf16),
            sd((n, CTX, D), bf16),
            sd((n, HEADS, PAD, CTX), bf16),
            sd((n, PAD, D), bf16),
            sd((n, PAD, HD), f32),
            sd(wshape, bf16),
        ],
        scratch_shapes=[pltpu.VMEM((HEADS, CTX, 2 * HD), bf16)],
        compiler_params=pltpu.CompilerParams(
            dimension_semantics=("arbitrary", "arbitrary"), vmem_limit_bytes=VLIM_FWD
        ),
        cost_estimate=pl.CostEstimate(
            flops=14_000_000_000, transcendentals=n * HEADS * PAD * CTX, bytes_accessed=40_000_000
        ),
        name="attention_forward",
    )(me.reshape(1), x, x, *parts)


def lane_mean(v):
    return jnp.sum(v, axis=-1, keepdims=True) * (1.0 / D)


NSUB = 1


def rows_body(ways, cnt_ref, x_ref, o_ref, li_ref, c_ref, *refs):
    parts, (sp_ref,
            out_ref, d1_ref, do_ref, keep_ref, send_ref, gs_ref, go_ref, gi_ref, gb_ref,
            gbs, dus, dfs, hbs, das, osc, *placed) = refs[:ways], refs[ways:]
    w_ref = placed[0] if placed else parts[0]
    me = cnt_ref[cnt_ref.shape[0] - 1]
    pieces, small = 2 * keep_ref.shape[0], 2 * gs_ref.shape[0]
    n, rb = pl.program_id(0), pl.program_id(1)
    first = jnp.logical_and(n == 0, rb == 0)
    last = jnp.logical_and(n == pl.num_programs(0) - 1, rb == NRBL - 1)

    @pl.when(first)
    def _():
        go_ref[...] = jnp.zeros_like(go_ref)
        gi_ref[...] = jnp.zeros_like(gi_ref)
        gb_ref[...] = jnp.zeros_like(gb_ref)
        gs_ref[...] = jnp.zeros_like(gs_ref)
        if placed:
            put_in_order(me, parts, w_ref)

    per = w_ref.shape[1] // 5
    wo = w_ref[:, 0:per].reshape(D, D)
    wi = w_ref[:, per : 3 * per].reshape(FF, D)
    wb = w_ref[:, 3 * per :].reshape(FF, D)
    gain1, shift1 = sp_ref[0:1], sp_ref[1:2]
    bias2, gain2, shift2 = sp_ref[4:5], sp_ref[5:6], sp_ref[6:7]
    bias1 = jnp.concatenate([sp_ref[2:3], sp_ref[3:4]], axis=1)
    size = RBL // NSUB
    sums = []

    def chain(part):
        rs = slice(part * size, (part + 1) * size)
        here = pl.ds(pl.multiple_of(rb * RBL, RBL) + part * size, size)
        osc[here] = o_ref[0, rs]
        rows = rb * RBL + part * size + lax.broadcasted_iota(jnp.int32, (size, 1), 0)
        valid = rows < SLOTS
        live = rows < CTX + cnt_ref[n]
        at = nt(o_ref[0, rs], wo)
        yield
        r1 = jnp.where(valid, x_ref[0, rs].astype(f32), 0.0) + at
        c1 = r1 - lane_mean(r1)
        is1 = lax.rsqrt(lane_mean(c1 * c1) + eps_norm)
        xh1 = c1 * is1
        h = xh1 * gain1 + shift1
        hb = h.astype(bf16)
        hbs[here] = hb
        yield
        u = nt(hb, wi)
        yield
        u = u + bias1
        ex = jnp.exp2((-0.7213475204444817 * u) * u)
        t = 1.0 / (1.0 + 0.23164189 * jnp.abs(u))
        poly = t * (0.127414796 + t * (-0.142248368 + t * (0.7107068705 + t * (-0.7265760135 + t * 0.5307027145))))
        tail = poly * ex
        phi = jnp.where(u >= 0.0, 1.0 - tail, tail)
        gb = (u * phi).astype(bf16)
        gbs[here] = gb
        dgelu = phi + u * ex * 0.3989422804014327
        yield
        r2 = nn(gb, wb)
        yield
        r2 = h + r2 + bias2
        c2 = r2 - lane_mean(r2)
        is2 = lax.rsqrt(lane_mean(c2 * c2) + eps_norm)
        xh2 = c2 * is2
        out_ref[0, rs] = jnp.where(live, xh2 * gain2 + shift2, 0.0).astype(bf16)
        dy = jnp.where(live, c_ref[0, rs].astype(f32), 0.0)
        s5 = jnp.sum(dy * xh2, axis=0, keepdims=True)
        s6 = jnp.sum(dy, axis=0, keepdims=True)
        e2 = dy * gain2
        d2 = (e2 - lane_mean(e2) - xh2 * lane_mean(e2 * xh2)) * is2
        df = d2.astype(bf16)
        dfs[here] = df
        s4 = jnp.sum(df.astype(f32), axis=0, keepdims=True)
        yield
        dg = nt(df, wb)
        yield
        du = (dg * dgelu).astype(bf16)
        dus[here] = du
        s2 = jnp.sum(du.astype(f32), axis=0, keepdims=True)
        yield
        dh = nn(du, wi)
        yield
        dh = d2 + dh
        s0 = jnp.sum(dh * xh1, axis=0, keepdims=True)
        s1 = jnp.sum(dh, axis=0, keepdims=True)
        e1 = dh * gain1
        d1 = (e1 - lane_mean(e1) - xh1 * lane_mean(e1 * xh1)) * is1
        d1_ref[0, rs] = d1
        da = d1.astype(bf16)
        das[here] = da
        sums.append((s0, s1, s2[:, :D], s2[:, D:], s4, s5, s6))
        yield
        dm = nn(da, wo)
        yield
        for h in range(HEADS):
            hs = slice(h * HD, (h + 1) * HD)
            li = li_ref[0, rs, h * (HD // HEADS) : h * (HD // HEADS) + 1]
            do_ref[0, rs, hs] = (dm[:, hs] * li).astype(bf16)

    chains = [chain(i) for i in range(NSUB)]
    for i, c in enumerate(chains):
        for _ in range(len(chains) - 1 - i):
            next(c)
    done = 0
    while done < len(chains):
        done = 0
        for c in chains:
            try:
                next(c)
            except StopIteration:
                done += 1
    for i in range(7):
        total_i = sums[0][i]
        for s in sums[1:]:
            total_i = total_i + s[i]
        gs_ref[i : i + 1] += total_i

    @pl.when(rb == NRBL - 1)
    def _():
        for target, left, right in ((gi_ref, dus, hbs), (gb_ref, gbs, dfs), (go_ref, das, osc)):
            target[...] += tn(left[...], right[...])

    def write(core):
        for p in range(pieces):
            out = keep_ref if p % 2 == core else send_ref
            if p < 2:
                high = gs_ref[...].astype(bf16)
                out[0, : small // 2] = high
                out[0, small // 2 : small] = (gs_ref[...] - high.astype(f32)).astype(bf16)
            else:
                out[p // 2, :small] = jnp.zeros((small, D), bf16)
            at = small
            for target in (gi_ref, gb_ref, go_ref):
                size = target.shape[0] // pieces
                out[p // 2, at : at + size] = target[p * size : (p + 1) * size].astype(bf16)
                at += size

    for core in range(2):
        pl.when(jnp.logical_and(last, me % 2 == core))(functools.partial(write, core))


def rows_pass(counts, x, o, li, cot, rest, sp, pieces):
    n = x.shape[0]
    placed = []
    if len(rest) > 1:
        placed = [pltpu.VMEM((2 * rest[0].shape[0],) + rest[0].shape[1:], bf16)]
    cut = (pieces // 2, 16 + (D + 2 * FF) // pieces, D)
    sd = jax.ShapeDtypeStruct
    blk = pl.BlockSpec((1, RBL, D), lambda i, r, c: (i, r, 0))
    const = lambda *s: pl.BlockSpec(s, lambda i, r, c: (0,) * len(s))
    return pl.pallas_call(
        functools.partial(rows_body, len(rest)),
        grid_spec=pltpu.PrefetchScalarGridSpec(
            num_scalar_prefetch=1,
            grid=(n, NRBL),
            in_specs=[
                blk,
                blk,
                pl.BlockSpec((1, RBL, HD), lambda i, r, c: (i, r, 0)),
                blk,
            ]
            + [const(*w.shape) for w in rest]
            + [const(8, D)],
            out_specs=[blk, blk, blk, const(*cut), const(*cut)],
            scratch_shapes=[
                pltpu.VMEM((8, D), f32),
                pltpu.VMEM((D, D), f32),
                pltpu.VMEM((FF, D), f32),
                pltpu.VMEM((FF, D), f32),
                pltpu.VMEM((PAD, FF), bf16),
                pltpu.VMEM((PAD, FF), bf16),
                pltpu.VMEM((PAD, D), bf16),
                pltpu.VMEM((PAD, D), bf16),
                pltpu.VMEM((PAD, D), bf16),
                pltpu.VMEM((PAD, D), bf16),
            ]
            + placed,
        ),
        out_shape=[
            sd((n, SLOTS, D), bf16),
            sd((n, SLOTS, D), f32),
            sd((n, PAD, D), bf16),
            sd(cut, bf16),
            sd(cut, bf16),
        ],
        compiler_params=pltpu.CompilerParams(
            dimension_semantics=("arbitrary", "arbitrary"), vmem_limit_bytes=VLIM_ROWS
        ),
        cost_estimate=pl.CostEstimate(
            flops=n * 18_000_000_000 // 2, transcendentals=n * PAD * FF * 2, bytes_accessed=n * 15_000_000
        ),
        name="rows_forward_backward",
    )(counts, x, o, li, cot, *rest, sp)


def attn_bwd_body(cut, *refs):
    x_ref, q_ref, k_ref, v_ref, e_ref, o_ref, do_ref, acc_ref, w_ref, *refs = refs
    (me_ref, other_ref), refs = (refs[:2], refs[2:]) if cut else ((None, None), refs)
    gi_ref, *outs = refs[:-4]
    dkt_ref, dvt_ref, gw_ref, xs_ref = refs[-4:]
    n, rb = pl.program_id(0), pl.program_id(1)

    @pl.when(jnp.logical_and(n == 0, rb == 0))
    def _():
        gw_ref[...] = jnp.zeros_like(gw_ref)

    @pl.when(rb == 0)
    def _():
        dkt_ref[...] = jnp.zeros_like(dkt_ref)
        dvt_ref[...] = jnp.zeros_like(dvt_ref)

    rows = rb * RBL + lax.broadcasted_iota(jnp.int32, (RBL, 1), 0)
    x = jnp.where(rows < SLOTS, x_ref[0].astype(f32), 0.0).astype(bf16)
    here = pl.ds(pl.multiple_of(rb * RBL, RBL), RBL)
    xs_ref[here] = x
    dqs = []
    for h in range(2):
        hs = slice(h * HD, (h + 1) * HD)
        do = do_ref[0, :, hs]
        t = jnp.sum(do.astype(f32) * o_ref[0, :, hs].astype(f32), axis=-1, keepdims=True)
        dp = nt(do, v_ref[0, :, hs])
        e = e_ref[0, h]
        ds = (e.astype(f32) * (dp - t)).astype(bf16)
        dqs.append(nn(ds, k_ref[0, :, hs]).astype(bf16))
        dvt_ref[hs] += tn(do, e)
        dkt_ref[hs] += tn(q_ref[0, :, hs], ds)
    dq = jnp.concatenate(dqs, axis=1)
    wq, wk, wv = (w_ref[:, i].reshape(2 * HD, D) for i in range(3))
    gw_ref[0] += tn(dq, x) * scaling
    gi_ref[0, here] = acc_ref[0] + nn(dq, wq) * scaling

    @pl.when(rb == NRBL - 1)
    def _():
        dkt, dvt = dkt_ref[...].astype(bf16), dvt_ref[...].astype(bf16)
        xc = xs_ref[0:CTX]
        gw_ref[1] += nn(dkt, xc)
        gw_ref[2] += nn(dvt, xc)
        gi_ref[0, 0:CTX] += tn(dkt, wk) + tn(dvt, wv)

    last = jnp.logical_and(n == pl.num_programs(0) - 1, rb == NRBL - 1)
    if not cut:

        @pl.when(last)
        def _():
            outs[0][...] = gw_ref[...]

        return

    def write(core):
        pieces, size = 2 * outs[0].shape[0], outs[0].shape[2]
        for p in range(pieces):
            out = outs[0] if p % 2 == core else outs[1]
            half, row = divmod(p * size, 2 * HD)
            for i in range(3):
                out[p // 2, i] = (gw_ref if half else other_ref)[i, row : row + size].astype(bf16)

    for core in range(2):
        pl.when(jnp.logical_and(last, me_ref[0] % 2 == core))(functools.partial(write, core))


def attn_bwd(pair, x, q, k, v, e, o, do, acc, wqkv, cut=()):
    n = x.shape[0]
    sd = jax.ShapeDtypeStruct
    ways = wqkv.shape[0]
    if ways > 1:
        wspec = pl.BlockSpec((ways // 2,) + wqkv.shape[1:], lambda i, r: (pair, 0, 0, 0))
    else:
        wspec = pl.BlockSpec((1, 3, 2 * HD, D), lambda i, r: (0, 0, pair, 0))
    heads = pl.BlockSpec((1, RBL, 2 * HD), lambda i, r: (i, r, pair))
    context = pl.BlockSpec((1, CTX, 2 * HD), lambda i, r: (i, 0, pair))
    rows = pl.BlockSpec((1, RBL, D), lambda i, r: (i, r, 0))
    grads = lambda shape: pl.BlockSpec(shape, lambda i, r: (0,) * len(shape))
    outs = [sd((cut[2] // 2, 3, D // cut[2], D), bf16)] * 2 if cut else [sd((3, 2 * HD, D), f32)]
    return pl.pallas_call(
        functools.partial(attn_bwd_body, bool(cut)),
        grid=(n, NRBL),
        in_specs=[
            rows,
            heads,
            context,
            context,
            pl.BlockSpec((1, 2, RBL, CTX), lambda i, r: (i, pair, r, 0)),
            heads,
            heads,
            rows,
            wspec,
        ]
        + ([pl.BlockSpec(memory_space=pltpu.SMEM), grads((3, 2 * HD, D))] if cut else []),
        out_specs=[pl.BlockSpec((1, PAD, D), lambda i, r: (i, 0, 0))] + [grads(g.shape) for g in outs],
        out_shape=[sd((n, SLOTS, D), f32)] + outs,
        scratch_shapes=[
            pltpu.VMEM((2 * HD, CTX), f32),
            pltpu.VMEM((2 * HD, CTX), f32),
            pltpu.VMEM((3, 2 * HD, D), f32),
            pltpu.VMEM((PAD, D), bf16),
        ],
        input_output_aliases={7: 0},
        compiler_params=pltpu.CompilerParams(
            dimension_semantics=("arbitrary", "arbitrary"), vmem_limit_bytes=VLIM_BWD
        ),
        cost_estimate=pl.CostEstimate(
            flops=9_000_000_000, transcendentals=0, bytes_accessed=24_000_000
        ),
        name="attention_backward",
    )(x, q, k, v, e, o, do, acc, wqkv, *([cut[0].reshape(1), cut[1]] if cut else []))


def adam_direction(first_new, second_new):
    return (first_new * (1.0 / (1.0 - beta_one**STEP))) / (
        jnp.sqrt(second_new * (1.0 / (1.0 - beta_two**STEP))) + eps_adam
    )


def rotate(grad, rows_basis, cols_basis, first_old, second_old):
    r = nn(tn(rows_basis, grad).astype(bf16), cols_basis)
    first_new = beta_one * first_old.astype(f32) + (1.0 - beta_one) * r
    second_new = beta_two * second_old.astype(f32) + (1.0 - beta_two) * r * r
    step = adam_direction(first_new, second_new).astype(bf16)
    return r.astype(bf16), nn(rows_basis, nt(step, cols_basis).astype(bf16)).astype(bf16)


def rotate_body(g_ref, a_ref, b_ref, m_ref, r_ref, u_ref):
    r_ref[...], u_ref[...] = rotate(g_ref[...], a_ref[...], b_ref[...], m_ref[0], m_ref[1])


def rotated_step(grad, rows_basis, cols_basis, moments):
    rows = grad.shape[0]
    sd = jax.ShapeDtypeStruct
    return pl.pallas_call(
        rotate_body,
        out_shape=[sd((rows, D), bf16), sd((rows, D), bf16)],
        compiler_params=pltpu.CompilerParams(vmem_limit_bytes=VLIM_STEP),
        cost_estimate=pl.CostEstimate(
            flops=4 * rows * D * (rows + D), transcendentals=rows * D, bytes_accessed=2 * rows * (rows + 5 * D)
        ),
        name="rotated_step",
    )(grad, rows_basis, cols_basis, moments)


def rotate_parts_body(me_ref, *refs):
    grads, a_ref, b_ref, olds, outs = refs[:2], refs[2], refs[3], refs[4:6], refs[6:10]
    g_ref, m_ref, r_ref, u_ref = refs[10:]
    me = me_ref[0]
    planes, inner, rows = len(outs), g_ref.shape[0], r_ref.shape[0]
    per = rows // (planes * inner)
    put_in_order(me & (inner - 1), grads, g_ref)
    put_in_order(me, olds, m_ref)
    r_ref[...], u_ref[...] = rotate(
        g_ref[...].reshape(rows, D), a_ref[...], b_ref[...],
        m_ref[:, 0].reshape(rows, D), m_ref[:, 1].reshape(rows, D),
    )
    n = g_ref.shape[1]
    for rel, out in enumerate(outs):
        row = pl.multiple_of((me ^ (rel * inner)) * per, per)
        out[0] = g_ref[row // n, pl.ds(pl.multiple_of(row % n, per), per)]
        out[1] = r_ref[pl.ds(row, per)]
        out[2] = u_ref[pl.ds(row, per)]


def rotated_step_parts(me, grads, rows_basis, cols_basis, olds, block):
    rows = rows_basis.shape[0]
    inner = 2 * grads[0].shape[0]
    count = 2 * olds[0].shape[0]
    per = rows // count
    full = lambda shape: pl.BlockSpec(shape, lambda i: (0,) * len(shape))
    return pl.pallas_call(
        rotate_parts_body,
        grid=(1,),
        in_specs=[pl.BlockSpec(memory_space=pltpu.SMEM)]
        + [full(g.shape) for g in grads]
        + [full(rows_basis.shape), full(cols_basis.shape)]
        + [pl.BlockSpec((count // 2, 2, per, D), lambda i: (0, 0, block, 0))] * 2,
        out_specs=[full((3, per, D))] * (count // inner),
        out_shape=[jax.ShapeDtypeStruct((3, per, D), bf16)] * (count // inner),
        scratch_shapes=[
            pltpu.VMEM((inner, rows // inner, D), bf16),
            pltpu.VMEM((count, 2, per, D), bf16),
            pltpu.VMEM((rows, D), bf16),
            pltpu.VMEM((rows, D), bf16),
        ],
        compiler_params=pltpu.CompilerParams(vmem_limit_bytes=VLIM_STEP),
        cost_estimate=pl.CostEstimate(
            flops=4 * rows * D * (rows + D), transcendentals=rows * D, bytes_accessed=2 * rows * (rows + 5 * D)
        ),
        name="rotated_step",
    )(me.reshape(1), *grads, rows_basis, cols_basis, *(pltpu.with_memory_space_constraint(v, pltpu.HBM) for v in olds))


class Net:
    def __init__(self, mesh):
        self.count = mesh.size
        self.bits = self.count.bit_length() - 1
        self.inner_bits = self.bits - 2
        self.inner = 1 << self.inner_bits
        self.me = lax.axis_index(axes)
        self.local = self.me & (self.inner - 1)
        self.plane = self.me >> self.inner_bits
        stages = [(0, 1)]
        while stages[-1][0] + stages[-1][1] < self.inner_bits:
            low = stages[-1][0] + stages[-1][1]
            stages.append((low, min(2, self.inner_bits - low)))
        self.stages = stages
        self.top = (self.inner_bits, 2)

    def swap(self, value, offset, targets=(0, 1, 2, 3), sources=(0, 1, 2, 3)):
        pairs = [(i, i ^ offset) for i in range(self.count)]
        pairs = [
            (i, j) for i, j in pairs
            if (i >> self.inner_bits) in sources and (j >> self.inner_bits) in targets
        ]
        return lax.ppermute(value, axes, pairs)

    def digit(self, stage):
        return (self.me >> stage[0]) & ((1 << stage[1]) - 1)

    def collect(self, value, stage):
        return [value] + [self.swap(value, rel << stage[0]) for rel in range(1, 1 << stage[1])]

    def widen(self, value, stage):
        return interleave(self.collect(value, stage))

    def cut(self, pick, stage):
        mine = self.digit(stage)
        return [pick(mine ^ rel) for rel in range(1 << stage[1])]

    def trade(self, terms, stage, targets=(0, 1, 2, 3), sources=(0, 1, 2, 3)):
        return list(terms[:1]) + [
            self.swap(term, rel << stage[0], targets, sources) for rel, term in enumerate(terms) if rel
        ]


def after(value, *earlier):
    return lax.optimization_barrier((value, earlier))[0]


def interleave(parts):
    value = jnp.stack(parts, axis=1)
    return value.reshape((-1,) + value.shape[2:])


def total(parts):
    parts = [p.astype(f32) for p in parts]
    while len(parts) > 1:
        parts = [a + b for a, b in zip(parts[0::2], parts[1::2])]
    return parts[0]


def take_at(value, index, axis):
    return lax.dynamic_index_in_dim(value, index, axis, keepdims=False)


def join_high(pair):
    half = pair.shape[0] // 2
    return pair[:half].astype(f32) + pair[half:].astype(f32)


def sum_cut_body(low, bits, small, me_ref, *refs):
    size = 1 << bits
    parts, terms = refs[:-size], refs[-size:]
    digit = (me_ref[0] >> low) & (size - 1)
    if small:
        whole = total([join_high(p[0, :small]) for p in parts])
        high = whole.astype(bf16)
        pair = jnp.concatenate([high, (whole - high.astype(f32)).astype(bf16)])
    for rel, term in enumerate(terms):
        for j in range(term.shape[0]):
            piece = j * size + (digit ^ rel)
            if small:
                term[j, :small] = pair
                term[j, small:] = total([p[piece, small:] for p in parts]).astype(bf16)
            else:
                term[j] = total([p[piece] for p in parts]).astype(bf16)


def sum_top_body(low, small, me_ref, *refs):
    parts, terms = refs[:-4], refs[-4:]
    plane = (me_ref[0] >> low) & 3
    for rel, term in enumerate(terms):
        goal = plane ^ rel
        if not small:
            piece = jnp.minimum(goal, 2)
            term[...] = total([p[0, piece] for p in parts]).astype(bf16)
            continue
        rows = term.shape[0] - small
        whole = total([join_high(p[0, :small]) for p in parts])
        high = whole.astype(bf16)
        term[:small] = jnp.concatenate([high, (whole - high.astype(f32)).astype(bf16)])

        def give(k):
            count = min(rows, parts[0].shape[1] - small - k * rows)
            begin = small + k * rows
            term[small : small + count] = total([p[0, begin : begin + count] for p in parts]).astype(bf16)
            if count < rows:
                term[small + count :] = jnp.zeros((rows - count, D), bf16)

        for k in range(3):
            pl.when(jnp.maximum(goal, 1) == k + 1)(functools.partial(give, k))


def deal(body, me, parts, term, count):
    full = lambda dims: pl.BlockSpec(dims, lambda i: (0,) * len(dims))
    return pl.pallas_call(
        body,
        grid=(1,),
        in_specs=[pl.BlockSpec(memory_space=pltpu.SMEM)] + [full(p.shape) for p in parts],
        out_specs=[full(term)] * count,
        out_shape=[pltpu.HBM(term, bf16)] * count,
        compiler_params=pltpu.CompilerParams(vmem_limit_bytes=VLIM_STEP),
        cost_estimate=pl.CostEstimate(
            flops=0, transcendentals=0, bytes_accessed=4 * len(parts) * parts[0].size
        ),
        name="sum_and_deal",
    )(me.reshape(1), *parts)


def sum_cut(net, parts, stage, small=0):
    size = 1 << stage[1]
    shape = parts[0].shape
    body = functools.partial(sum_cut_body, *stage, small)
    return deal(body, net.me, parts, (shape[0] // size,) + shape[1:], size)


def sum_top(net, parts, rows, small=0):
    body = functools.partial(sum_top_body, net.top[0], small)
    return deal(body, net.me, parts, (small + rows, D), 4)


def place_body(me_ref, *refs):
    *parts, out = refs
    put_in_order(me_ref[0] & (out.shape[0] - 1), parts, out)


def place(me, parts):
    size = len(parts) * parts[0].shape[0]
    shape = jax.ShapeDtypeStruct((size,) + parts[0].shape[1:], parts[0].dtype)
    return pl.pallas_call(
        place_body,
        in_specs=[pl.BlockSpec(memory_space=pltpu.SMEM)]
        + [pl.BlockSpec(memory_space=pltpu.VMEM)] * len(parts),
        out_specs=pl.BlockSpec(memory_space=pltpu.VMEM),
        out_shape=shape,
        compiler_params=pltpu.CompilerParams(vmem_limit_bytes=24 * 1024 * 1024),
        cost_estimate=pl.CostEstimate(flops=0, transcendentals=0, bytes_accessed=4 * shape.size),
        name="place",
    )(me.reshape(1), *parts)


def finish_body(low, me_ref, *refs):
    attn, ffn = refs[:4], refs[4:8]
    moments_ref, weights_ref, grad_ref, new_ref, out_ref = refs[8:]
    plane = (me_ref[0] >> low) & 3
    per = attn[0].shape[1]
    rows = 8 * per

    def choose(parts, plain, kind):
        value = parts[0][kind].astype(f32)
        for rel in range(1, 4):
            value = jnp.where(plane == (plain ^ rel), parts[rel][kind].astype(f32), value)
        return value.astype(bf16)

    row = lax.broadcasted_iota(jnp.int32, (rows, rows), 0)
    source = lax.broadcasted_iota(jnp.int32, (rows, rows), 1)
    group, slot = row // 8, row % 8
    wanted = jnp.where(
        slot < 4, slot * per + group, (4 + 2 * ((slot - 4) // 2)) * per + 2 * group + slot % 2
    )
    order = jnp.where(source == wanted, 1.0, 0.0).astype(bf16)

    def plain(kind):
        parts = [choose(attn, b, kind) for b in range(4)] + [choose(ffn, f, kind) for f in (1, 2)]
        return nn(order, jnp.concatenate(parts))

    grad_ref[...] = plain(0)
    turned = plain(1)
    new_ref[0] = beta_one * moments_ref[0] + (1.0 - beta_one) * turned
    new_ref[1] = beta_two * moments_ref[1] + (1.0 - beta_two) * turned * turned
    out_ref[...] = weights_ref[...] - rate_mats * plain(2)


def finish(net, attn, ffn, moments, weights):
    full = lambda shape: pl.BlockSpec(shape, lambda i: (0,) * len(shape))
    arrays = [*attn, *ffn, moments, weights]
    outs = [weights, moments, weights]
    return pl.pallas_call(
        functools.partial(finish_body, net.top[0]),
        grid=(1,),
        in_specs=[pl.BlockSpec(memory_space=pltpu.SMEM)] + [full(v.shape) for v in arrays],
        out_specs=[full(v.shape) for v in outs],
        out_shape=[jax.ShapeDtypeStruct(v.shape, f32) for v in outs],
        compiler_params=pltpu.CompilerParams(vmem_limit_bytes=VLIM_STEP),
        cost_estimate=pl.CostEstimate(flops=50_000_000, transcendentals=0, bytes_accessed=3_000_000),
        name="finish",
    )(net.me.reshape(1), *arrays)


def by_index(parts, index):
    return [
        functools.reduce(
            lambda rest, r: jnp.where(index == (b ^ r), parts[r], rest), range(1, len(parts)), parts[0]
        )
        for b in range(len(parts))
    ]


def on_device(mesh, features, cotangent, counts, weights, small_params, moments_old, small_moments,
              basis_attn, basis_ffn, basis_cols):
    net = Net(mesh)
    per = weights.shape[0] // 8
    everyone = net.stages + [net.top]

    def by_matrix(stacked):
        groups = stacked.reshape(per, 8, D)
        return (
            jnp.transpose(groups[:, 0:4], (1, 0, 2)),
            groups[:, 4:6].reshape(2 * per, D),
            groups[:, 6:8].reshape(2 * per, D),
        )

    def stacked(attn, inner, outer):
        return jnp.concatenate(
            [jnp.stack(attn, axis=1), inner.reshape(per, 2, D), outer.reshape(per, 2, D)], axis=1
        ).reshape(8 * per, D)

    inner = net.inner
    n_attn, n_ffn = D // inner, FF // inner
    ffn_of = lambda plane: jnp.clip(plane - 1, 0, 1)
    stages, top = net.stages, net.top

    own_attn, own_in, own_out = by_matrix(weights.astype(bf16))
    first = own_attn[None, 0:3]
    rest = jnp.concatenate([own_attn[3], own_in, own_out])[None]
    olds = [by_matrix(moments_old[i].astype(bf16)) for i in range(2)]
    old_attn = jnp.stack([m[0] for m in olds], axis=1)
    old_ffn = jnp.stack([jnp.stack([m[1], m[2]]) for m in olds], axis=1)
    old_terms = net.cut(
        lambda d: jnp.concatenate([take_at(old_ffn, ffn_of(d), 0), take_at(old_attn, d, 0)], axis=1), top
    )
    mine = ffn_of(net.plane)
    bases = (
        take_at(basis_attn, net.plane, 0).astype(bf16),
        take_at(basis_cols, net.plane, 0).astype(bf16),
        take_at(basis_cols, 4 + mine, 0).astype(bf16),
    )
    sp = jnp.concatenate([small_params.reshape(7, D), jnp.zeros((1, D), f32)])
    counts_me = jnp.concatenate([counts, net.me.reshape(1)])

    whole_tiles = per % 16 == 0
    order = list(reversed(everyone))
    first = interleave(net.collect(first, order[0]))
    rest_parts = net.collect(after(rest, first), order[0])
    for i, stage in enumerate(order[1:]):
        first_parts = net.collect(first, stage)
        if i == 0:
            first_parts, bases, old_terms, sp, counts_me = after(
                (first_parts, bases, old_terms, sp, counts_me), first
            )
        if stage is not order[-1]:
            first = interleave(first_parts)
            rest_parts, first = after((rest_parts, first), first_parts)
            rest = interleave(rest_parts)
            rest_parts = net.collect(rest, stage)
    if not whole_tiles:
        first_parts = [jnp.transpose(place(net.me, first_parts), (1, 0, 2, 3)).reshape(1, 3, D, D)]
    first_parts, sp, counts_me = lax.optimization_barrier((first_parts, sp, counts_me, rest, bases, old_terms))[:3]
    old_parts = net.trade(after(old_terms, rest), top)
    q, k, v, e, o, li, wqkv = attn_fwd(features, first_parts, net.me)
    rest_parts, old_parts = after((rest_parts, old_parts), o)
    rest, olds = interleave(rest_parts), jnp.stack(old_parts)
    for stage in reversed(stages[2:]):
        olds = net.widen(olds, stage)
    rest_parts = net.collect(after(rest, olds), order[-1])
    old_parts = net.collect(olds, stages[1])
    if not whole_tiles:
        rest = place(net.me, rest_parts)
        rest_parts = [
            jnp.concatenate(
                [rest[:, lo * per : hi * per].reshape(-1, D) for lo, hi in ((0, 1), (1, 3), (3, 5))]
            )[None]
        ]
    output, d1, do, *terms = rows_pass(
        counts_me, features, o, li, cotangent, after(rest_parts, olds), sp, inner
    )

    n_small = 16
    terms, old_parts = after((terms, old_parts), output)
    early_parts = net.trade(terms, stages[0])
    olds = interleave(old_parts)
    early_parts = after(early_parts, olds)
    for stage in stages[2:]:
        early_parts = net.trade(sum_cut(net, early_parts, stage, n_small), stage)
    terms = sum_cut(net, early_parts, stages[1], n_small)
    early_parts = net.trade(terms, stages[1])
    old_parts = net.collect(olds, stages[0])
    back = functools.partial(attn_bwd, x=features, q=q, k=k, v=v, e=e, o=o, do=do)
    acc, gw0 = back(0, acc=d1, wqkv=after(wqkv, terms, olds))
    early_parts, old_parts = after((early_parts, old_parts), gw0)
    top_terms = sum_top(net, early_parts, n_ffn, n_small)
    top_parts = net.trade(top_terms, top)
    grad_input, *terms = back(1, acc=acc, wqkv=after(wqkv, top_terms, old_parts), cut=(net.me, gw0, inner))

    terms, top_parts = lax.optimization_barrier((terms, top_parts))
    late_parts = net.trade(terms, stages[0])
    ffn = total([p[n_small:] for p in top_parts]).astype(bf16)
    ffn_parts = net.collect(ffn[None], stages[-1])
    late_parts = after(late_parts, ffn)
    for stage in stages[2:]:
        late_parts = net.trade(sum_cut(net, late_parts, stage), stage)
    terms = sum_cut(net, late_parts, stages[1])
    late_parts = net.trade(terms, stages[1])
    a_ffn = take_at(after(basis_ffn, terms), mine, 0).astype(bf16)
    early_part, ffn_parts, a_ffn = lax.optimization_barrier((late_parts[1], ffn_parts, a_ffn))
    wide = interleave(ffn_parts)
    late_parts, wide = lax.optimization_barrier((late_parts[:1] + [early_part] + late_parts[2:], wide))
    terms = sum_top(net, late_parts, n_attn)
    late_parts = net.trade(terms, top, (0, 1, 2))
    wide = after(wide, terms)
    ffn_parts = net.collect(wide, stages[len(stages) - 2])
    for stage in reversed(stages[:-2]):
        ffn_parts = net.collect(interleave(ffn_parts), stage)

    if whole_tiles:
        back_ffn = rotated_step_parts(net.me, ffn_parts, a_ffn, bases[2], old_parts, 0)
    else:
        olds = jnp.transpose(place(net.me, old_parts), (1, 0, 2, 3))
        full = place(net.me, ffn_parts).reshape(FF, D)
        both = rotated_step(full, a_ffn, bases[2], olds[:, :, : 2 * per].reshape(2, FF, D))
        back_ffn = take_at(jnp.stack([full, *both]).reshape(3, 4, inner, 2 * per, D), net.local, 2)
        back_ffn = net.cut(lambda d: take_at(back_ffn, d, 1), top)
    late_parts = after(late_parts, back_ffn)
    attn = total(late_parts).astype(bf16)
    attn = jnp.where(net.plane == 3, ffn[:n_attn], attn)[None]
    gs = total([join_high(p[:n_small]) for p in after(top_parts, attn)])
    grad_small = gs[0:7].reshape(-1)
    small_first = beta_one * small_moments[0] + (1.0 - beta_one) * grad_small
    small_second = beta_two * small_moments[1] + (1.0 - beta_two) * grad_small * grad_small
    small_new = small_params - rate_small * adam_direction(small_first, small_second)
    small_moments_new = jnp.stack([small_first, small_second])
    for stage in reversed(stages[1:]):
        attn_parts = net.collect(attn, stage)
        attn_parts, small_new, small_moments_new = lax.optimization_barrier(
            (attn_parts, small_new, small_moments_new)
        )
        attn = interleave(attn_parts)
    attn_parts = net.collect(attn, stages[0])
    back_ffn = net.trade(back_ffn, top, sources=(1, 2))
    if whole_tiles:
        back_attn = rotated_step_parts(net.me, attn_parts, bases[0], bases[1], old_parts, 2)
    else:
        full = place(net.me, attn_parts).reshape(D, D)
        both = rotated_step(full, bases[0], bases[1], olds[:, :, 2 * per :].reshape(2, D, D))
        back_attn = take_at(jnp.stack([full, *both]).reshape(3, 4, inner, per, D), net.local, 2)
        back_attn = net.cut(lambda d: take_at(back_attn, d, 1), top)
    back_ffn = after(back_ffn, back_attn)
    back_attn = net.trade(back_attn, top)
    if whole_tiles:
        grad_weights, moments_new, weights_new = finish(net, back_attn, back_ffn, moments_old, weights)
    else:
        back_attn = by_index(back_attn, net.plane)
        back_ffn = by_index(back_ffn, net.plane)
        grad_weights, rotated, update = (
            stacked([part[i] for part in back_attn], back_ffn[1][i], back_ffn[2][i]).astype(f32) for i in range(3)
        )
        moments_new = jnp.stack(
            [
                beta_one * moments_old[0] + (1.0 - beta_one) * rotated,
                beta_two * moments_old[1] + (1.0 - beta_two) * rotated * rotated,
            ]
        )
        weights_new = weights - rate_mats * update
    return (
        output,
        grad_input,
        grad_weights,
        moments_new,
        weights_new,
        grad_small,
        small_moments_new,
        small_new,
    )


def solution(mesh):
    rows = P(("dp", "fsdp"), None)
    blocks = P(("dp", "fsdp"), None, None)
    pair = P(None, ("dp", "fsdp"), None)
    return jax.shard_map(
        lambda *arrays: on_device(mesh, *arrays),
        mesh=mesh,
        in_specs=(blocks, blocks, P(("dp", "fsdp")), rows, P(), pair, P(), P(), P(), P()),
        out_specs=(blocks, blocks, rows, pair, rows, P(), P(), P()),
        check_vma=False,
    )
```

profile of v0, /device:TPU:0, one launch (start us, length us, event | category | flops | bytes accessed | tf_op | source)
XLA Modules:
  0.0 213.5 jit_solution(11245290140216004838)
XLA Ops:
  1.7 5.1 %collective-permute-start.2 = (bf16[1,3,16,512]{3,2,1,0:T(8,128)(2,1)S(1)}, bf16[1,3,16,512]{3,2,1,0:T(8,128)(2,1)S(1)}, u32[]{:S(2)}, u32[]{:S(2)}) collective-permute-start(bf16[1,3,16,512]{3,2,1,0:T(8,128)(2,1)S(1)} %get-tuple-element.311), channel_id=1, source_target_pairs={{0,24},{1,25},{2,26},{3,27},{4,28},{5,29},{6,30},{7,31},{8,16},{9,... | collective-permute-start | bytes 147464 | tf_op jit(solution)/shard_map/ppermute | solution.py:555
  9.6 2.2 %collective-permute-done.1 = bf16[1,3,16,512]{3,2,1,0:T(8,128)(2,1)S(1)} collective-permute-done((bf16[1,3,16,512]{3,2,1,0:T(8,128)(2,1)S(1)}, bf16[1,3,16,512]{3,2,1,0:T(8,128)(2,1)S(1)}, u32[]{:S(2)}, u32[]{:S(2)}) %collective-permute-start.1) | collective-permute-done | bytes 49184 | tf_op jit(solution)/shard_map/ppermute | solution.py:555
  11.8 2.5 %collective-permute-start.8 = (bf16[4,3,16,512]{3,2,1,0:T(8,128)(2,1)S(1)}, bf16[4,3,16,512]{3,2,1,0:T(8,128)(2,1)S(1)}, u32[]{:S(2)}, u32[]{:S(2)}) collective-permute-start(bf16[4,3,16,512]{3,2,1,0:T(8,128)(2,1)S(1)} %maximum_bitcast_fusion.3), channel_id=1, source_target_pairs={{0,6},{1,7},{2,4},{3,5},{4,2},{5,3},{6,0},{7,1},{8,14},{9,15},{10,... | collective-permute-start | bytes 589832 | tf_op jit(solution)/shard_map/ppermute | solution.py:555
  15.5 2.9 %fusion.3 = (bf16[512,512]{1,0:T(8,128)(2,1)}, bf16[512,512]{1,0:T(8,128)(2,1)S(1)}, bf16[512,512]{1,0:T(8,128)(2,1)S(1)}) fusion(f32[6,512,512]{2,1,0:T(8,128)} %param.19, s32[]{:T(128)S(6)} %select_n.41, s32[]{:T(128)S(6)} %select_n.40, f32[4,512,512]{2,1,0:T(8,128)} %param.17, s32[]{:T(128)S(6)} %select_n.39), kind=kLoop, calls=%fused_computation.10 | loop fusion | bytes 3145740 | tf_op jit(solution)/shard_map/convert_element_type | solution.py:786
  20.4 2.3 %collective-permute-start.3 = (bf16[1,80,512]{2,1,0:T(8,128)(2,1)S(1)}, bf16[1,80,512]{2,1,0:T(8,128)(2,1)S(1)}, u32[]{:S(2)}, u32[]{:S(2)}) collective-permute-start(bf16[1,80,512]{2,1,0:T(8,128)(2,1)S(1)} %maximum_bitcast_fusion.4), channel_id=1, source_target_pairs={{0,8},{1,9},{2,10},{3,11},{4,12},{5,13},{6,14},{7,15},{8,0},{9,1},... | collective-permute-start | bytes 245768 | tf_op jit(solution)/shard_map/ppermute | solution.py:555
  24.7 2.3 %collective-permute-done.4 = bf16[1,80,512]{2,1,0:T(8,128)(2,1)S(1)} collective-permute-done((bf16[1,80,512]{2,1,0:T(8,128)(2,1)S(1)}, bf16[1,80,512]{2,1,0:T(8,128)(2,1)S(1)}, u32[]{:S(2)}, u32[]{:S(2)}) %collective-permute-start.4) | collective-permute-done | bytes 81952 | tf_op jit(solution)/shard_map/ppermute | solution.py:555
  27.3 2.5 %collective-permute-start.12 = (bf16[4,80,512]{2,1,0:T(8,128)(2,1)S(1)}, bf16[4,80,512]{2,1,0:T(8,128)(2,1)S(1)}, u32[]{:S(2)}, u32[]{:S(2)}) collective-permute-start(bf16[4,80,512]{2,1,0:T(8,128)(2,1)S(1)} %maximum_bitcast_fusion.1), channel_id=1, source_target_pairs={{0,6},{1,7},{2,4},{3,5},{4,2},{5,3},{6,0},{7,1},{8,14},{9,15},{10,... | collective-permute-start | bytes 983048 | tf_op jit(solution)/shard_map/ppermute | solution.py:555
  30.8 2.1 collective-permute-start.14
  35.0 23.3 %attention_forward.1 = (bf16[2,1152,512]{2,1,0:T(8,128)(2,1)}, bf16[2,1024,512]{2,1,0:T(8,128)(2,1)}, bf16[2,1024,512]{2,1,0:T(8,128)(2,1)}, bf16[2,4,1152,1024]...) custom-call(s32[1]{0:T(128)} %bitcast.25.refs_0_.me_ref.refs_9_, ...), custom_call_target="tpu_custom_call" | custom-call | flops 14000000000 | bytes 40000000 | tf_op jit(solution)/shard_map/attention_forward/pallas_call | solution.py:103
  58.7 2.5 %collective-permute-start.19 = (bf16[4,2,48,512]{3,2,1,0:T(8,128)(2,1)S(1)}, bf16[4,2,48,512]{3,2,1,0:T(8,128)(2,1)S(1)}, u32[]{:S(2)}, u32[]{:S(2)}) collective-permute-start(bf16[4,2,48,512]{3,2,1,0:T(8,128)(2,1)S(1)} %pad_maximum_fusion.3), channel_id=1, source_target_pairs={{0,6},{1,7},{2,4},{3,5},{4,2},{5,3},{6,0},{7,1},{8,14},{9,15},{10,... | collective-permute-start | bytes 1179656 | tf_op jit(solution)/shard_map/ppermute | solution.py:555
  62.2 37.2 %rows_forward_backward.1 = (bf16[2,1128,512]{2,1,0:T(8,128)(2,1)}, f32[2,1128,512]{2,1,0:T(8,128)}, bf16[2,1152,512]{2,1,0:T(8,128)(2,1)}, bf16[4,336,512]{2,1,0:T(8,128)(2,1)S(1)}, bf16[4,336,512]{2,1,0:T(8,128)(2,1)S(1)}) custom-call(s32[3]{0:T(128)S(1)} %pad_add_fusion.cnt_ref, bf16[2,1128,512]{2,1,0:T(8,128)(2,1)} %refs_0_.3, ...), custom_call_target="tpu_custom_call" | custom-call | flops 17999998976 | bytes 30000000 | tf_op jit(solution)/shard_map/rows_forward_backward/pallas_call | solution.py:295
  100.3 2.3 %collective-permute-done.20.refs_1_ = bf16[4,336,512]{2,1,0:T(8,128)(2,1)S(1)} collective-permute-done((bf16[4,336,512]{2,1,0:T(8,128)(2,1)S(1)}, bf16[4,336,512]{2,1,0:T(8,128)(2,1)S(1)}, u32[]{:S(2)}, u32[]{:S(2)}) %collective-permute-start.20) | collective-permute-done | bytes 1376288 | tf_op jit(solution)/shard_map/ppermute | solution.py:555
  107.4 18.3 %attention_backward.2 = (f32[2,1128,512]{2,1,0:T(8,128)}, f32[3,256,512]{2,1,0:T(8,128)S(1)}) custom-call(bf16[2,1128,512]{2,1,0:T(8,128)(2,1)} %refs_0_.3, bf16[2,1152,512]{2,1,0:T(8,128)(2,1)} %get-tuple-element.186.refs_1_, bf16[2,1024,512]{2,1,0:T(8,128)(2,1)S(1)} %copy-done, ...), custom_call_target="tpu_custom_call", output_to_operand_aliasing={{0}: (7, {})} | custom-call | flops 8999999488 | bytes 24000000 | tf_op jit(solution)/shard_map/attention_backward/pallas_call | solution.py:418
  127.1 2.3 %collective-permute-start.26 = (bf16[144,512]{1,0:T(8,128)(2,1)}, bf16[144,512]{1,0:T(8,128)(2,1)S(1)}, u32[]{:S(2)}, u32[]{:S(2)}) collective-permute-start(bf16[144,512]{1,0:T(8,128)(2,1)} %get-tuple-element.216), channel_id=1, source_target_pairs={{0,16},{1,17},{2,18},{3,19},{4,20},{5,21},{6,22},{7,23},{8,24},{9,... | collective-permute-start | bytes 442376 | tf_op jit(solution)/shard_map/ppermute | solution.py:555
  131.5 18.3 %attention_backward.3 = (f32[2,1128,512]{2,1,0:T(8,128)}, bf16[4,3,64,512]{3,2,1,0:T(8,128)(2,1)S(1)}, bf16[4,3,64,512]{3,2,1,0:T(8,128)(2,1)S(1)}) custom-call(bf16[2,1128,512]{2,1,0:T(8,128)(2,1)} %refs_0_.3, bf16[2,1152,512]{2,1,0:T(8,128)(2,1)} %get-tuple-element.186.refs_1_, bf16[2,1024,512]{2,1,0:T(8,128)(2,1)S(1)} %copy-done, ...), custom_call_target="tpu_custom_call", output_to_operand_aliasing={{0}: (7, {})} | custom-call | flops 8999999488 | bytes 24000000 | tf_op jit(solution)/shard_map/attention_backward/pallas_call | solution.py:418
  150.0 2.5 %collective-permute-start.32 = (bf16[1,128,512]{2,1,0:T(8,128)(2,1)S(1)}, bf16[1,128,512]{2,1,0:T(8,128)(2,1)S(1)}, u32[]{:S(2)}, u32[]{:S(2)}) collective-permute-start(bf16[1,128,512]{2,1,0:T(8,128)(2,1)S(1)} %bitcast.125), channel_id=1, source_target_pairs={{0,6},{1,7},{2,4},{3,5},{4,2},{5,3},{6,0},{7,1},{8,14},{9,15},{10,... | collective-permute-start | bytes 393224 | tf_op jit(solution)/shard_map/ppermute | solution.py:555
  157.5 2.2 %collective-permute-start.34 = (bf16[1,3,64,512]{3,2,1,0:T(8,128)(2,1)}, bf16[1,3,64,512]{3,2,1,0:T(8,128)(2,1)S(1)}, u32[]{:S(2)}, u32[]{:S(2)}) collective-permute-start(bf16[1,3,64,512]{3,2,1,0:T(8,128)(2,1)} %get-tuple-element.235), channel_id=1, source_target_pairs={{0,6},{1,7},{2,4},{3,5},{4,2},{5,3},{6,0},{7,1},{8,14},{9,15},{10,... | collective-permute-start | bytes 589832 | tf_op jit(solution)/shard_map/ppermute | solution.py:555
  159.7 2.5 %fusion.refs_2_ = bf16[1024,1024]{1,0:T(8,128)(2,1)S(1)} fusion(f32[2,1024,1024]{2,1,0:T(8,128)} %param.18, s32[]{:T(128)S(6)} %min.16), kind=kLoop, calls=%fused_computation.1 | loop fusion | bytes 4194308 | tf_op jit(solution)/shard_map/convert_element_type | solution.py:854
  165.2 2.4 %collective-permute-done.33.refs_2_ = bf16[1,3,64,512]{3,2,1,0:T(8,128)(2,1)S(1)} collective-permute-done((bf16[1,3,64,512]{3,2,1,0:T(8,128)(2,1)}, bf16[1,3,64,512]{3,2,1,0:T(8,128)(2,1)S(1)}, u32[]{:S(2)}, u32[]{:S(2)}) %collective-permute-start.33) | collective-permute-done | bytes 196640 | tf_op jit(solution)/shard_map/ppermute | solution.py:555
  175.2 6.9 %rotated_step.2 = (bf16[3,32,512]{2,1,0:T(8,128)(2,1)S(1)}, bf16[3,32,512]{2,1,0:T(8,128)(2,1)S(1)}, bf16[3,32,512]{2,1,0:T(8,128)(2,1)S(1)}, bf16[3,32,512]{2,1,0:T(8,128)(2,1)S(1)}) custom-call(s32[1]{0:T(128)} %bitcast.25.refs_0_.me_ref.refs_9_, bf16[4,128,512]{2,1,0:T(8,128)(2,1)} %maximum_bitcast_fusion.refs_0_, ...), custom_call_target="tpu_custom_call" | custom-call | flops 3221225472 | bytes 7340032 | tf_op jit(solution)/shard_map/rotated_step/pallas_call | solution.py:510
  182.2 2.3 %collective-permute-start.41 = (bf16[1,64,512]{2,1,0:T(8,128)(2,1)S(1)}, bf16[1,64,512]{2,1,0:T(8,128)(2,1)S(1)}, u32[]{:S(2)}, u32[]{:S(2)}) collective-permute-start(bf16[1,64,512]{2,1,0:T(8,128)(2,1)S(1)} %fusion.5), channel_id=1, source_target_pairs={{0,6},{1,7},{2,4},{3,5},{4,2},{5,3},{6,0},{7,1},{8,14},{9,15},{10,... | collective-permute-start | bytes 196616 | tf_op jit(solution)/shard_map/ppermute | solution.py:555
  194.4 3.4 %rotated_step.3 = (bf16[3,16,512]{2,1,0:T(8,128)(2,1)S(1)}, bf16[3,16,512]{2,1,0:T(8,128)(2,1)S(1)}, bf16[3,16,512]{2,1,0:T(8,128)(2,1)S(1)}, bf16[3,16,512]{2,1,0:T(8,128)(2,1)S(1)}) custom-call(s32[1]{0:T(128)} %bitcast.25.refs_0_.me_ref.refs_9_, bf16[4,64,512]{2,1,0:T(8,128)(2,1)S(1)} %maximum_bitcast_fusion.2.refs_0_, ...), custom_call_target="tpu_custom_call" | custom-call | flops 1073741824 | bytes 3145728 | tf_op jit(solution)/shard_map/rotated_step/pallas_call | solution.py:510
  197.8 7.5 %collective-permute-start.43 = (bf16[3,16,512]{2,1,0:T(8,128)(2,1)S(1)}, bf16[3,16,512]{2,1,0:T(8,128)(2,1)S(1)}, u32[]{:S(2)}, u32[]{:S(2)}) collective-permute-start(bf16[3,16,512]{2,1,0:T(8,128)(2,1)S(1)} %get-tuple-element.270), channel_id=1, source_target_pairs={{0,8},{1,9},{2,10},{3,11},{4,12},{5,13},{6,14},{7,15},{8,0},{9,1},... | collective-permute-start | bytes 147464 | tf_op jit(solution)/shard_map/ppermute | solution.py:555
  207.8 3.8 %collective-permute-done.44.refs_2_ = bf16[3,16,512]{2,1,0:T(8,128)(2,1)S(1)} collective-permute-done((bf16[3,16,512]{2,1,0:T(8,128)(2,1)S(1)}, bf16[3,16,512]{2,1,0:T(8,128)(2,1)S(1)}, u32[]{:S(2)}, u32[]{:S(2)}) %collective-permute-start.44) | collective-permute-done | bytes 49184 | tf_op jit(solution)/shard_map/ppermute | solution.py:555
  (186 shorter events, 52.6 us)
Async XLA Ops:
  27.3 31.0 %collective-permute-start.12 = (bf16[4,80,512]{2,1,0:T(8,128)(2,1)S(1)}, bf16[4,80,512]{2,1,0:T(8,128)(2,1)S(1)}, u32[]{:S(2)}, u32[]{:S(2)}) collective-permute-start(bf16[4,80,512]{2,1,0:T(8,128)(2,1)S(1)} %maximum_bitcast_fusion.1), channel_id=1, source_target_pairs={{0,6},{1,7},{2,4},{3,5},{4,2},{5,3},{6,0},{7,1},{8,14},{9,15},{10,... | collective-permute-start | bytes 983048 | tf_op jit(solution)/shard_map/ppermute | solution.py:555
  29.8 28.6 %collective-permute-start.11 = (bf16[4,80,512]{2,1,0:T(8,128)(2,1)S(1)}, bf16[4,80,512]{2,1,0:T(8,128)(2,1)S(1)}, u32[]{:S(2)}, u32[]{:S(2)}) collective-permute-start(bf16[4,80,512]{2,1,0:T(8,128)(2,1)S(1)} %maximum_bitcast_fusion.1), channel_id=1, source_target_pairs={{0,4},{1,5},{2,6},{3,7},{4,0},{5,1},{6,2},{7,3},{8,12},{9,13},{10,... | collective-permute-start | bytes 983048 | tf_op jit(solution)/shard_map/ppermute | solution.py:555
  30.3 28.1 %collective-permute-start.10 = (bf16[4,80,512]{2,1,0:T(8,128)(2,1)S(1)}, bf16[4,80,512]{2,1,0:T(8,128)(2,1)S(1)}, u32[]{:S(2)}, u32[]{:S(2)}) collective-permute-start(bf16[4,80,512]{2,1,0:T(8,128)(2,1)S(1)} %maximum_bitcast_fusion.1), channel_id=1, source_target_pairs={{0,2},{1,3},{2,0},{3,1},{4,6},{5,7},{6,4},{7,5},{8,10},{9,11},{10,... | collective-permute-start | bytes 983048 | tf_op jit(solution)/shard_map/ppermute | solution.py:555
  30.8 27.5 %collective-permute-start.14 = (bf16[2,48,512]{2,1,0:T(8,128)(2,1)S(1)}, bf16[2,48,512]{2,1,0:T(8,128)(2,1)S(1)}, u32[]{:S(2)}, u32[]{:S(2)}) collective-permute-start(bf16[2,48,512]{2,1,0:T(8,128)(2,1)S(1)} %pad_maximum_fusion.6), channel_id=1, source_target_pairs={{0,16},{1,17},{2,18},{3,19},{4,20},{5,21},{6,22},{7,23},{8,24},{9,... | collective-permute-start | bytes 294920 | tf_op jit(solution)/shard_map/ppermute | solution.py:555
  32.9 25.4 %collective-permute-start.15 = (bf16[2,48,512]{2,1,0:T(8,128)(2,1)S(1)}, bf16[2,48,512]{2,1,0:T(8,128)(2,1)S(1)}, u32[]{:S(2)}, u32[]{:S(2)}) collective-permute-start(bf16[2,48,512]{2,1,0:T(8,128)(2,1)S(1)} %pad_maximum_fusion.7), channel_id=1, source_target_pairs={{0,24},{1,25},{2,26},{3,27},{4,28},{5,29},{6,30},{7,31},{8,16},{9,... | collective-permute-start | bytes 294920 | tf_op jit(solution)/shard_map/ppermute | solution.py:555
  58.7 40.7 %collective-permute-start.19 = (bf16[4,2,48,512]{3,2,1,0:T(8,128)(2,1)S(1)}, bf16[4,2,48,512]{3,2,1,0:T(8,128)(2,1)S(1)}, u32[]{:S(2)}, u32[]{:S(2)}) collective-permute-start(bf16[4,2,48,512]{3,2,1,0:T(8,128)(2,1)S(1)} %pad_maximum_fusion.3), channel_id=1, source_target_pairs={{0,6},{1,7},{2,4},{3,5},{4,2},{5,3},{6,0},{7,1},{8,14},{9,15},{10,... | collective-permute-start | bytes 1179656 | tf_op jit(solution)/shard_map/ppermute | solution.py:555
  61.2 38.2 %collective-permute-start.18 = (bf16[4,2,48,512]{3,2,1,0:T(8,128)(2,1)S(1)}, bf16[4,2,48,512]{3,2,1,0:T(8,128)(2,1)S(1)}, u32[]{:S(2)}, u32[]{:S(2)}) collective-permute-start(bf16[4,2,48,512]{3,2,1,0:T(8,128)(2,1)S(1)} %pad_maximum_fusion.3), channel_id=1, source_target_pairs={{0,4},{1,5},{2,6},{3,7},{4,0},{5,1},{6,2},{7,3},{8,12},{9,13},{10,... | collective-permute-start | bytes 1179656 | tf_op jit(solution)/shard_map/ppermute | solution.py:555
  61.7 37.7 %collective-permute-start.17 = (bf16[4,2,48,512]{3,2,1,0:T(8,128)(2,1)S(1)}, bf16[4,2,48,512]{3,2,1,0:T(8,128)(2,1)S(1)}, u32[]{:S(2)}, u32[]{:S(2)}) collective-permute-start(bf16[4,2,48,512]{3,2,1,0:T(8,128)(2,1)S(1)} %pad_maximum_fusion.3), channel_id=1, source_target_pairs={{0,2},{1,3},{2,0},{3,1},{4,6},{5,7},{6,4},{7,5},{8,10},{9,11},{10,... | collective-permute-start | bytes 1179656 | tf_op jit(solution)/shard_map/ppermute | solution.py:555
  99.7 26.0 %collective-permute-start.24 = (bf16[16,2,48,512]{3,2,1,0:T(8,128)(2,1)S(1)}, bf16[16,2,48,512]{3,2,1,0:T(8,128)(2,1)S(1)}, u32[]{:S(2)}, u32[]{:S(2)}) collective-permute-start(bf16[16,2,48,512]{3,2,1,0:T(8,128)(2,1)S(1)} %bitcast.120), channel_id=1, source_target_pairs={{0,1},{1,0},{2,3},{3,2},{4,5},{5,4},{6,7},{7,6},{8,9},{9,8},{10,11... | collective-permute-start | bytes 4718600 | tf_op jit(solution)/shard_map/ppermute | solution.py:555
  103.9 21.8 %collective-permute-start.21 = (bf16[1,336,512]{2,1,0:T(8,128)(2,1)}, bf16[1,336,512]{2,1,0:T(8,128)(2,1)S(1)}, u32[]{:S(2)}, u32[]{:S(2)}) collective-permute-start(bf16[1,336,512]{2,1,0:T(8,128)(2,1)} %get-tuple-element.204), channel_id=1, source_target_pairs={{0,2},{1,3},{2,0},{3,1},{4,6},{5,7},{6,4},{7,5},{8,10},{9,11},{10,... | collective-permute-start | bytes 1032200 | tf_op jit(solution)/shard_map/ppermute | solution.py:555
  105.4 20.4 %collective-permute-start.22 = (bf16[1,336,512]{2,1,0:T(8,128)(2,1)}, bf16[1,336,512]{2,1,0:T(8,128)(2,1)S(1)}, u32[]{:S(2)}, u32[]{:S(2)}) collective-permute-start(bf16[1,336,512]{2,1,0:T(8,128)(2,1)} %get-tuple-element.205), channel_id=1, source_target_pairs={{0,4},{1,5},{2,6},{3,7},{4,0},{5,1},{6,2},{7,3},{8,12},{9,13},{10,... | collective-permute-start | bytes 1032200 | tf_op jit(solution)/shard_map/ppermute | solution.py:555
  106.9 18.8 %collective-permute-start.23 = (bf16[1,336,512]{2,1,0:T(8,128)(2,1)}, bf16[1,336,512]{2,1,0:T(8,128)(2,1)S(1)}, u32[]{:S(2)}, u32[]{:S(2)}) collective-permute-start(bf16[1,336,512]{2,1,0:T(8,128)(2,1)} %get-tuple-element.206), channel_id=1, source_target_pairs={{0,6},{1,7},{2,4},{3,5},{4,2},{5,3},{6,0},{7,1},{8,14},{9,15},{10,... | collective-permute-start | bytes 1032200 | tf_op jit(solution)/shard_map/ppermute | solution.py:555
  127.1 22.7 %collective-permute-start.25 = (bf16[144,512]{1,0:T(8,128)(2,1)}, bf16[144,512]{1,0:T(8,128)(2,1)S(1)}, u32[]{:S(2)}, u32[]{:S(2)}) collective-permute-start(bf16[144,512]{1,0:T(8,128)(2,1)} %get-tuple-element.215), channel_id=1, source_target_pairs={{0,8},{1,9},{2,10},{3,11},{4,12},{5,13},{6,14},{7,15},{8,0},{9,1},... | collective-permute-start | bytes 442376 | tf_op jit(solution)/shard_map/ppermute | solution.py:555
  127.1 22.7 %collective-permute-start.26 = (bf16[144,512]{1,0:T(8,128)(2,1)}, bf16[144,512]{1,0:T(8,128)(2,1)S(1)}, u32[]{:S(2)}, u32[]{:S(2)}) collective-permute-start(bf16[144,512]{1,0:T(8,128)(2,1)} %get-tuple-element.216), channel_id=1, source_target_pairs={{0,16},{1,17},{2,18},{3,19},{4,20},{5,21},{6,22},{7,23},{8,24},{9,... | collective-permute-start | bytes 442376 | tf_op jit(solution)/shard_map/ppermute | solution.py:555
  129.4 20.4 %collective-permute-start.27 = (bf16[144,512]{1,0:T(8,128)(2,1)}, bf16[144,512]{1,0:T(8,128)(2,1)S(1)}, u32[]{:S(2)}, u32[]{:S(2)}) collective-permute-start(bf16[144,512]{1,0:T(8,128)(2,1)} %get-tuple-element.217), channel_id=1, source_target_pairs={{0,24},{1,25},{2,26},{3,27},{4,28},{5,29},{6,30},{7,31},{8,16},{9,... | collective-permute-start | bytes 442376 | tf_op jit(solution)/shard_map/ppermute | solution.py:555
  153.4 10.9 %collective-permute-start.29 = (bf16[1,3,64,512]{3,2,1,0:T(8,128)(2,1)}, bf16[1,3,64,512]{3,2,1,0:T(8,128)(2,1)S(1)}, u32[]{:S(2)}, u32[]{:S(2)}) collective-permute-start(bf16[1,3,64,512]{3,2,1,0:T(8,128)(2,1)} %get-tuple-element.233), channel_id=1, source_target_pairs={{0,2},{1,3},{2,0},{3,1},{4,6},{5,7},{6,4},{7,5},{8,10},{9,11},{10,... | collective-permute-start | bytes 589832 | tf_op jit(solution)/shard_map/ppermute | solution.py:555
  156.6 10.9 %collective-permute-start.33 = (bf16[1,3,64,512]{3,2,1,0:T(8,128)(2,1)}, bf16[1,3,64,512]{3,2,1,0:T(8,128)(2,1)S(1)}, u32[]{:S(2)}, u32[]{:S(2)}) collective-permute-start(bf16[1,3,64,512]{3,2,1,0:T(8,128)(2,1)} %get-tuple-element.234), channel_id=1, source_target_pairs={{0,4},{1,5},{2,6},{3,7},{4,0},{5,1},{6,2},{7,3},{8,12},{9,13},{10,... | collective-permute-start | bytes 589832 | tf_op jit(solution)/shard_map/ppermute | solution.py:555
  157.5 10.8 %collective-permute-start.34 = (bf16[1,3,64,512]{3,2,1,0:T(8,128)(2,1)}, bf16[1,3,64,512]{3,2,1,0:T(8,128)(2,1)S(1)}, u32[]{:S(2)}, u32[]{:S(2)}) collective-permute-start(bf16[1,3,64,512]{3,2,1,0:T(8,128)(2,1)} %get-tuple-element.235), channel_id=1, source_target_pairs={{0,6},{1,7},{2,4},{3,5},{4,2},{5,3},{6,0},{7,1},{8,14},{9,15},{10,... | collective-permute-start | bytes 589832 | tf_op jit(solution)/shard_map/ppermute | solution.py:555
  169.0 13.1 %collective-permute-start.35 = (bf16[64,512]{1,0:T(8,128)(2,1)}, bf16[64,512]{1,0:T(8,128)(2,1)S(1)}, u32[]{:S(2)}, u32[]{:S(2)}) collective-permute-start(bf16[64,512]{1,0:T(8,128)(2,1)} %get-tuple-element.247), channel_id=1, source_target_pairs={{0,8},{1,9},{2,10},{3,11},{4,12},{5,13},{6,14},{7,15},{8,0},{9,1},... | collective-permute-start | bytes 196616 | tf_op jit(solution)/shard_map/ppermute | solution.py:555
  170.9 11.2 %collective-permute-start.36 = (bf16[64,512]{1,0:T(8,128)(2,1)}, bf16[64,512]{1,0:T(8,128)(2,1)S(1)}, u32[]{:S(2)}, u32[]{:S(2)}) collective-permute-start(bf16[64,512]{1,0:T(8,128)(2,1)} %get-tuple-element.248), channel_id=1, source_target_pairs={{0,16},{1,17},{2,18},{3,19},{4,20},{5,21},{6,22},{7,23},{16,0},{17... | collective-permute-start | bytes 196616 | tf_op jit(solution)/shard_map/ppermute | solution.py:555
  191.0 15.3 %collective-permute-start.46 = (bf16[3,32,512]{2,1,0:T(8,128)(2,1)S(1)}, bf16[3,32,512]{2,1,0:T(8,128)(2,1)S(1)}, u32[]{:S(2)}, u32[]{:S(2)}) collective-permute-start(bf16[3,32,512]{2,1,0:T(8,128)(2,1)S(1)} %get-tuple-element.254), channel_id=1, source_target_pairs={{8,0},{9,1},{10,2},{11,3},{12,4},{13,5},{14,6},{15,7},{16,24},{17,... | collective-permute-start | bytes 294920 | tf_op jit(solution)/shard_map/ppermute | solution.py:555
  192.5 15.3 %collective-permute-start.47 = (bf16[3,32,512]{2,1,0:T(8,128)(2,1)S(1)}, bf16[3,32,512]{2,1,0:T(8,128)(2,1)S(1)}, u32[]{:S(2)}, u32[]{:S(2)}) collective-permute-start(bf16[3,32,512]{2,1,0:T(8,128)(2,1)S(1)} %get-tuple-element.255), channel_id=1, source_target_pairs={{8,24},{9,25},{10,26},{11,27},{12,28},{13,29},{14,30},{15,31},{16,... | collective-permute-start | bytes 294920 | tf_op jit(solution)/shard_map/ppermute | solution.py:555
  193.8 14.0 %collective-permute-start.48 = (bf16[3,32,512]{2,1,0:T(8,128)(2,1)S(1)}, bf16[3,32,512]{2,1,0:T(8,128)(2,1)S(1)}, u32[]{:S(2)}, u32[]{:S(2)}) collective-permute-start(bf16[3,32,512]{2,1,0:T(8,128)(2,1)S(1)} %get-tuple-element.256), channel_id=1, source_target_pairs={{8,16},{9,17},{10,18},{11,19},{12,20},{13,21},{14,22},{15,23},{16,... | collective-permute-start | bytes 294920 | tf_op jit(solution)/shard_map/ppermute | solution.py:555
  197.8 9.9 %collective-permute-start.43 = (bf16[3,16,512]{2,1,0:T(8,128)(2,1)S(1)}, bf16[3,16,512]{2,1,0:T(8,128)(2,1)S(1)}, u32[]{:S(2)}, u32[]{:S(2)}) collective-permute-start(bf16[3,16,512]{2,1,0:T(8,128)(2,1)S(1)} %get-tuple-element.270), channel_id=1, source_target_pairs={{0,8},{1,9},{2,10},{3,11},{4,12},{5,13},{6,14},{7,15},{8,0},{9,1},... | collective-permute-start | bytes 147464 | tf_op jit(solution)/shard_map/ppermute | solution.py:555
  (48 other events, 428.6 us)
where the time goes:
time: 214 us
  Pallas kernels  113 us (53%)
  starting transfers between devices  64.6 us (30%)
  waiting for transfers between devices  18.3 us (9%)
  local copies, waits for them, and re-layouts  9.91 us (5%)
  other arithmetic  6.39 us (3%)
    ppermute x49, starting transfers between devices, swap(): return lax.ppermute(value, axes, pairs)  64.6 us
    pallas_call x1, Pallas kernels, rows_pass(): pl.pallas_call(functools.partial(rows_body, len(rest)), grid_spec=pltpu.P...  37.2 us
    pallas_call x2, Pallas kernels, attn_bwd(): pl.pallas_call(functools.partial(attn_bwd_body, bool(cut)), grid=(n, NRBL...  36.6 us
    pallas_call x1, Pallas kernels, attn_fwd(): pl.pallas_call(functools.partial(attn_fwd_body, len(parts)), grid=(n, NRB...  23.3 us
    ppermute x49, waiting for transfers between devices, swap(): return lax.ppermute(value, axes, pairs)  18.3 us
    pallas_call x2, Pallas kernels, rotated_step_parts(): pl.pallas_call(rotate_parts_body, grid=(1,), in_specs=[pl.BlockSpec(memor...  10.2 us
  transfers between devices with their start and end apart: 49, of which 10 were waited for; matrix products, arithmetic and copies ran while one was open for 6% of the time, Pallas kernels for 51%

commit v1 on v0

--- a/solution.py
+++ b/solution.py
@@ -780,11 +780,6 @@
         lambda d: jnp.concatenate([take_at(old_ffn, ffn_of(d), 0), take_at(old_attn, d, 0)], axis=1), top
     )
     mine = ffn_of(net.plane)
-    bases = (
-        take_at(basis_attn, net.plane, 0).astype(bf16),
-        take_at(basis_cols, net.plane, 0).astype(bf16),
-        take_at(basis_cols, 4 + mine, 0).astype(bf16),
-    )
     sp = jnp.concatenate([small_params.reshape(7, D), jnp.zeros((1, D), f32)])
     counts_me = jnp.concatenate([counts, net.me.reshape(1)])
 
@@ -794,18 +789,16 @@
     rest_parts = net.collect(after(rest, first), order[0])
     for i, stage in enumerate(order[1:]):
         first_parts = net.collect(first, stage)
-        if i == 0:
-            first_parts, bases, old_terms, sp, counts_me = after(
-                (first_parts, bases, old_terms, sp, counts_me), first
-            )
         if stage is not order[-1]:
             first = interleave(first_parts)
-            rest_parts, first = after((rest_parts, first), first_parts)
+            rest_parts, first, old_terms, sp, counts_me = after(
+                (rest_parts, first, old_terms, sp, counts_me), first_parts
+            )
             rest = interleave(rest_parts)
             rest_parts = net.collect(rest, stage)
     if not whole_tiles:
         first_parts = [jnp.transpose(place(net.me, first_parts), (1, 0, 2, 3)).reshape(1, 3, D, D)]
-    first_parts, sp, counts_me = lax.optimization_barrier((first_parts, sp, counts_me, rest, bases, old_terms))[:3]
+    first_parts, sp, counts_me = lax.optimization_barrier((first_parts, sp, counts_me, rest, old_terms))[:3]
     old_parts = net.trade(after(old_terms, rest), top)
     q, k, v, e, o, li, wqkv = attn_fwd(features, first_parts, net.me)
     rest_parts, old_parts = after((rest_parts, old_parts), o)
@@ -851,51 +844,55 @@
         late_parts = net.trade(sum_cut(net, late_parts, stage), stage)
     terms = sum_cut(net, late_parts, stages[1])
     late_parts = net.trade(terms, stages[1])
-    a_ffn = take_at(after(basis_ffn, terms), mine, 0).astype(bf16)
-    early_part, ffn_parts, a_ffn = lax.optimization_barrier((late_parts[1], ffn_parts, a_ffn))
+    a_ffn, b_ffn = after((basis_ffn, basis_cols), terms)
+    a_ffn, b_ffn = take_at(a_ffn, mine, 0).astype(bf16), take_at(b_ffn, 4 + mine, 0).astype(bf16)
+    early_part, ffn_parts, a_ffn, b_ffn = lax.optimization_barrier((late_parts[1], ffn_parts, a_ffn, b_ffn))
     wide = interleave(ffn_parts)
     late_parts, wide = lax.optimization_barrier((late_parts[:1] + [early_part] + late_parts[2:], wide))
     terms = sum_top(net, late_parts, n_attn)
-    late_parts = net.trade(terms, top, (0, 1, 2))
+    late_parts = net.trade(terms, top)
     wide = after(wide, terms)
     ffn_parts = net.collect(wide, stages[len(stages) - 2])
     for stage in reversed(stages[:-2]):
         ffn_parts = net.collect(interleave(ffn_parts), stage)
 
     if whole_tiles:
-        back_ffn = rotated_step_parts(net.me, ffn_parts, a_ffn, bases[2], old_parts, 0)
+        back_ffn = rotated_step_parts(net.me, ffn_parts, a_ffn, b_ffn, old_parts, 0)
     else:
         olds = jnp.transpose(place(net.me, old_parts), (1, 0, 2, 3))
         full = place(net.me, ffn_parts).reshape(FF, D)
-        both = rotated_step(full, a_ffn, bases[2], olds[:, :, : 2 * per].reshape(2, FF, D))
+        both = rotated_step(full, a_ffn, b_ffn, olds[:, :, : 2 * per].reshape(2, FF, D))
         back_ffn = take_at(jnp.stack([full, *both]).reshape(3, 4, inner, 2 * per, D), net.local, 2)
         back_ffn = net.cut(lambda d: take_at(back_ffn, d, 1), top)
     late_parts = after(late_parts, back_ffn)
     attn = total(late_parts).astype(bf16)
     attn = jnp.where(net.plane == 3, ffn[:n_attn], attn)[None]
     gs = total([join_high(p[:n_small]) for p in after(top_parts, attn)])
+    a_attn, b_attn = after((basis_attn, basis_cols), attn)
+    a_attn, b_attn = (take_at(basis, net.plane, 0).astype(bf16) for basis in (a_attn, b_attn))
+    for stage in reversed(stages[1:]):
+        attn_parts = net.collect(attn, stage)
+        attn_parts, gs, a_attn, b_attn = lax.optimization_barrier((attn_parts, gs, a_attn, b_attn))
+        attn = interleave(attn_parts)
+    attn_parts = net.collect(attn, stages[0])
+    back_ffn = net.trade(back_ffn, top)
+    if whole_tiles:
+        back_attn = rotated_step_parts(net.me, attn_parts, a_attn, b_attn, old_parts, 2)
+    else:
+        full = place(net.me, attn_parts).reshape(D, D)
+        both = rotated_step(full, a_attn, b_attn, olds[:, :, 2 * per :].reshape(2, D, D))
+        back_attn = take_at(jnp.stack([full, *both]).reshape(3, 4, inner, per, D), net.local, 2)
+        back_attn = net.cut(lambda d: take_at(back_attn, d, 1), top)
+    back_ffn, gs = after((back_ffn, gs), back_attn)
+    back_attn = net.trade(back_attn, top)
     grad_small = gs[0:7].reshape(-1)
     small_first = beta_one * small_moments[0] + (1.0 - beta_one) * grad_small
     small_second = beta_two * small_moments[1] + (1.0 - beta_two) * grad_small * grad_small
     small_new = small_params - rate_small * adam_direction(small_first, small_second)
     small_moments_new = jnp.stack([small_first, small_second])
-    for stage in reversed(stages[1:]):
-        attn_parts = net.collect(attn, stage)
-        attn_parts, small_new, small_moments_new = lax.optimization_barrier(
-            (attn_parts, small_new, small_moments_new)
-        )
-        attn = interleave(attn_parts)
-    attn_parts = net.collect(attn, stages[0])
-    back_ffn = net.trade(back_ffn, top, sources=(1, 2))
-    if whole_tiles:
-        back_attn = rotated_step_parts(net.me, attn_parts, bases[0], bases[1], old_parts, 2)
-    else:
-        full = place(net.me, attn_parts).reshape(D, D)
-        both = rotated_step(full, bases[0], bases[1], olds[:, :, 2 * per :].reshape(2, D, D))
-        back_attn = take_at(jnp.stack([full, *both]).reshape(3, 4, inner, per, D), net.local, 2)
-        back_attn = net.cut(lambda d: take_at(back_attn, d, 1), top)
-    back_ffn = after(back_ffn, back_attn)
-    back_attn = net.trade(back_attn, top)
+    back_attn, small_new, small_moments_new = lax.optimization_barrier(
+        (back_attn, small_new, small_moments_new)
+    )
     if whole_tiles:
         grad_weights, moments_new, weights_new = finish(net, back_attn, back_ffn, moments_old, weights)
     else:

time: 214 us -> 217 us (1.014)
  Pallas kernels: 113 us -> 124 us
  starting transfers between devices: 64.6 us -> 55.5 us
  waiting for transfers between devices: 18.3 us -> 22.8 us
  local copies, waits for them, and re-layouts: 9.91 us -> 7.07 us
    pallas_call x2, Pallas kernels: 36.6 us -> 47.4 us  [attn_bwd(): pl.pallas_call(functools.partial(attn_bwd_body, bool(cut)), grid=(n, NRBL...]
    ppermute x49, starting transfers between devices: 64.6 us -> 55.5 us  [swap(): return lax.ppermute(value, axes, pairs)]
    ppermute x49, waiting for transfers between devices: 18.3 us -> 22.8 us  [swap(): return lax.ppermute(value, axes, pairs)]
    slice x4 -> x0, local copies, waits for them, and re-layouts: 2.86 us -> none  [join_high(): return pair[:half].astype(f32) + pair[half:].astype(f32)]
    convert_element_type x2 -> x4, local copies, waits for them, and re-layouts: 5.37 us -> 6.43 us  [the longest x2 2.59 us: on_device(): take_at(basis, net.plane, 0).astype(bf16)]
  transfers between devices with their start and end apart: 49 -> 49, of which waited for: 10 -> 12; matrix products, arithmetic and copies ran while one was open for 6% -> 5% of each run, Pallas kernels for 51% -> 56%
where the time goes in v1:
time: 217 us; the launch traced here: 216 us
  Pallas kernels  124 us (57%)
  starting transfers between devices  55.5 us (26%)
  waiting for transfers between devices  22.8 us (11%)
  local copies, waits for them, and re-layouts  7.07 us (3%)
  other arithmetic  5.55 us (3%)
    ppermute x49, starting transfers between devices, swap(): return lax.ppermute(value, axes, pairs)  55.5 us
    pallas_call x2, Pallas kernels, attn_bwd(): pl.pallas_call(functools.partial(attn_bwd_body, bool(cut)), grid=(n, NRBL...  47.4 us
    pallas_call x1, Pallas kernels, rows_pass(): pl.pallas_call(functools.partial(rows_body, len(rest)), grid_spec=pltpu.P...  37.4 us
    pallas_call x1, Pallas kernels, attn_fwd(): pl.pallas_call(functools.partial(attn_fwd_body, len(parts)), grid=(n, NRB...  23.3 us
    ppermute x49, waiting for transfers between devices, swap(): return lax.ppermute(value, axes, pairs)  22.8 us
    pallas_call x2, Pallas kernels, rotated_step_parts(): pl.pallas_call(rotate_parts_body, grid=(1,), in_specs=[pl.BlockSpec(memor...  10.2 us
  transfers between devices with their start and end apart: 49, of which 12 were waited for; matrix products, arithmetic and copies ran while one was open for 5% of the time, Pallas kernels for 56%

profile of v1, /device:TPU:0, one launch (start us, length us, event | category | flops | bytes accessed | tf_op | source)
XLA Modules:
  0.0 216.4 jit_solution(8983291947135302338)
XLA Ops:
  1.7 3.1 %collective-permute-start = (bf16[1,3,16,512]{3,2,1,0:T(8,128)(2,1)S(1)}, bf16[1,3,16,512]{3,2,1,0:T(8,128)(2,1)S(1)}, u32[]{:S(2)}, u32[]{:S(2)}) collective-permute-start(bf16[1,3,16,512]{3,2,1,0:T(8,128)(2,1)S(1)} %get-tuple-element.313), channel_id=1, source_target_pairs={{0,8},{1,9},{2,10},{3,11},{4,12},{5,13},{6,14},{7,15},{8,0},{9,1},... | collective-permute-start | bytes 147464 | tf_op jit(solution)/shard_map/ppermute | solution.py:555
  4.8 2.6 %collective-permute-start.1 = (bf16[1,3,16,512]{3,2,1,0:T(8,128)(2,1)S(1)}, bf16[1,3,16,512]{3,2,1,0:T(8,128)(2,1)S(1)}, u32[]{:S(2)}, u32[]{:S(2)}) collective-permute-start(bf16[1,3,16,512]{3,2,1,0:T(8,128)(2,1)S(1)} %get-tuple-element.313), channel_id=1, source_target_pairs={{0,16},{1,17},{2,18},{3,19},{4,20},{5,21},{6,22},{7,23},{8,24},{9,... | collective-permute-start | bytes 147464 | tf_op jit(solution)/shard_map/ppermute | solution.py:555
  10.7 2.6 %collective-permute-done.2 = bf16[1,3,16,512]{3,2,1,0:T(8,128)(2,1)S(1)} collective-permute-done((bf16[1,3,16,512]{3,2,1,0:T(8,128)(2,1)S(1)}, bf16[1,3,16,512]{3,2,1,0:T(8,128)(2,1)S(1)}, u32[]{:S(2)}, u32[]{:S(2)}) %collective-permute-start.2) | collective-permute-done | bytes 49184 | tf_op jit(solution)/shard_map/ppermute | solution.py:555
  18.3 2.5 %collective-permute-done.6 = bf16[4,3,16,512]{3,2,1,0:T(8,128)(2,1)S(1)} collective-permute-done((bf16[4,3,16,512]{3,2,1,0:T(8,128)(2,1)S(1)}, bf16[4,3,16,512]{3,2,1,0:T(8,128)(2,1)S(1)}, u32[]{:S(2)}, u32[]{:S(2)}) %collective-permute-start.6) | collective-permute-done | bytes 196640 | tf_op jit(solution)/shard_map/ppermute | solution.py:555
  21.7 2.4 %collective-permute-done.7 = bf16[4,3,16,512]{3,2,1,0:T(8,128)(2,1)S(1)} collective-permute-done((bf16[4,3,16,512]{3,2,1,0:T(8,128)(2,1)S(1)}, bf16[4,3,16,512]{3,2,1,0:T(8,128)(2,1)S(1)}, u32[]{:S(2)}, u32[]{:S(2)}) %collective-permute-start.7) | collective-permute-done | bytes 196640 | tf_op jit(solution)/shard_map/ppermute | solution.py:555
  24.3 2.7 %collective-permute-done.5 = bf16[1,80,512]{2,1,0:T(8,128)(2,1)S(1)} collective-permute-done((bf16[1,80,512]{2,1,0:T(8,128)(2,1)S(1)}, bf16[1,80,512]{2,1,0:T(8,128)(2,1)S(1)}, u32[]{:S(2)}, u32[]{:S(2)}) %collective-permute-start.5) | collective-permute-done | bytes 81952 | tf_op jit(solution)/shard_map/ppermute | solution.py:555
  32.3 2.7 %collective-permute-start.15 = (bf16[2,48,512]{2,1,0:T(8,128)(2,1)S(1)}, bf16[2,48,512]{2,1,0:T(8,128)(2,1)S(1)}, u32[]{:S(2)}, u32[]{:S(2)}) collective-permute-start(bf16[2,48,512]{2,1,0:T(8,128)(2,1)S(1)} %pad_maximum_fusion.8), channel_id=1, source_target_pairs={{0,24},{1,25},{2,26},{3,27},{4,28},{5,29},{6,30},{7,31},{8,16},{9,... | collective-permute-start | bytes 294920 | tf_op jit(solution)/shard_map/ppermute | solution.py:555
  35.0 23.3 %attention_forward.1 = (bf16[2,1152,512]{2,1,0:T(8,128)(2,1)}, bf16[2,1024,512]{2,1,0:T(8,128)(2,1)}, bf16[2,1024,512]{2,1,0:T(8,128)(2,1)}, bf16[2,4,1152,1024]...) custom-call(s32[1]{0:T(128)} %bitcast.27.refs_0_.me_ref.refs_9_, ...), custom_call_target="tpu_custom_call" | custom-call | flops 14000000000 | bytes 40000000 | tf_op jit(solution)/shard_map/attention_forward/pallas_call | solution.py:103
  62.3 37.4 %rows_forward_backward.1 = (bf16[2,1128,512]{2,1,0:T(8,128)(2,1)}, f32[2,1128,512]{2,1,0:T(8,128)}, bf16[2,1152,512]{2,1,0:T(8,128)(2,1)}, bf16[4,336,512]{2,1,0:T(8,128)(2,1)S(1)}, bf16[4,336,512]{2,1,0:T(8,128)(2,1)S(1)}) custom-call(s32[3]{0:T(128)S(1)} %pad_add_fusion.cnt_ref, bf16[2,1128,512]{2,1,0:T(8,128)(2,1)} %refs_0_.3, ...), custom_call_target="tpu_custom_call" | custom-call | flops 17999998976 | bytes 30000000 | tf_op jit(solution)/shard_map/rows_forward_backward/pallas_call | solution.py:295
  100.5 2.3 %collective-permute-done.20.refs_1_ = bf16[4,336,512]{2,1,0:T(8,128)(2,1)S(1)} collective-permute-done((bf16[4,336,512]{2,1,0:T(8,128)(2,1)S(1)}, bf16[4,336,512]{2,1,0:T(8,128)(2,1)S(1)}, u32[]{:S(2)}, u32[]{:S(2)}) %collective-permute-start.20) | collective-permute-done | bytes 1376288 | tf_op jit(solution)/shard_map/ppermute | solution.py:555
  107.6 29.1 %attention_backward.2 = (f32[2,1128,512]{2,1,0:T(8,128)}, f32[3,256,512]{2,1,0:T(8,128)S(1)}) custom-call(bf16[2,1128,512]{2,1,0:T(8,128)(2,1)} %refs_0_.3, bf16[2,1152,512]{2,1,0:T(8,128)(2,1)} %get-tuple-element.184.refs_1_, bf16[2,1024,512]{2,1,0:T(8,128)(2,1)S(1)} %copy-done, ...), custom_call_target="tpu_custom_call", output_to_operand_aliasing={{0}: (7, {})} | custom-call | flops 8999999488 | bytes 24000000 | tf_op jit(solution)/shard_map/attention_backward/pallas_call | solution.py:418
  138.1 1.7 collective-permute-start.26
  139.8 2.7 %collective-permute-start.27 = (bf16[144,512]{1,0:T(8,128)(2,1)}, bf16[144,512]{1,0:T(8,128)(2,1)S(1)}, u32[]{:S(2)}, u32[]{:S(2)}) collective-permute-start(bf16[144,512]{1,0:T(8,128)(2,1)} %get-tuple-element.215), channel_id=1, source_target_pairs={{0,24},{1,25},{2,26},{3,27},{4,28},{5,29},{6,30},{7,31},{8,16},{9,... | collective-permute-start | bytes 442376 | tf_op jit(solution)/shard_map/ppermute | solution.py:555
  142.5 18.3 %attention_backward.3 = (f32[2,1128,512]{2,1,0:T(8,128)}, bf16[4,3,64,512]{3,2,1,0:T(8,128)(2,1)S(1)}, bf16[4,3,64,512]{3,2,1,0:T(8,128)(2,1)S(1)}) custom-call(bf16[2,1128,512]{2,1,0:T(8,128)(2,1)} %refs_0_.3, bf16[2,1152,512]{2,1,0:T(8,128)(2,1)} %get-tuple-element.184.refs_1_, bf16[2,1024,512]{2,1,0:T(8,128)(2,1)S(1)} %copy-done, ...), custom_call_target="tpu_custom_call", output_to_operand_aliasing={{0}: (7, {})} | custom-call | flops 8999999488 | bytes 24000000 | tf_op jit(solution)/shard_map/attention_backward/pallas_call | solution.py:418
  168.2 2.5 %fusion.refs_2_ = bf16[1024,1024]{1,0:T(8,128)(2,1)S(1)} fusion(f32[2,1024,1024]{2,1,0:T(8,128)} %param.18, s32[]{:T(128)S(6)} %min.20), kind=kLoop, calls=%fused_computation.1 | loop fusion | bytes 4194308 | tf_op jit(solution)/shard_map/convert_element_type | solution.py:848
  174.5 3.7 %collective-permute-done.33.refs_2_ = bf16[1,3,64,512]{3,2,1,0:T(8,128)(2,1)S(1)} collective-permute-done((bf16[1,3,64,512]{3,2,1,0:T(8,128)(2,1)}, bf16[1,3,64,512]{3,2,1,0:T(8,128)(2,1)S(1)}, u32[]{:S(2)}, u32[]{:S(2)}) %collective-permute-start.33) | collective-permute-done | bytes 196640 | tf_op jit(solution)/shard_map/ppermute | solution.py:555
  179.9 1.7 collective-permute-start.36
  181.6 2.7 %collective-permute-start.37 = (bf16[64,512]{1,0:T(8,128)(2,1)}, bf16[64,512]{1,0:T(8,128)(2,1)S(1)}, u32[]{:S(2)}, u32[]{:S(2)}) collective-permute-start(bf16[64,512]{1,0:T(8,128)(2,1)} %get-tuple-element.248), channel_id=1, source_target_pairs={{0,24},{1,25},{2,26},{3,27},{4,28},{5,29},{6,30},{7,31},{8,16},{9,... | collective-permute-start | bytes 196616 | tf_op jit(solution)/shard_map/ppermute | solution.py:555
  184.3 6.7 %rotated_step.2 = (bf16[3,32,512]{2,1,0:T(8,128)(2,1)S(1)}, bf16[3,32,512]{2,1,0:T(8,128)(2,1)S(1)}, bf16[3,32,512]{2,1,0:T(8,128)(2,1)S(1)}, bf16[3,32,512]{2,1,0:T(8,128)(2,1)S(1)}) custom-call(s32[1]{0:T(128)} %bitcast.27.refs_0_.me_ref.refs_9_, bf16[4,128,512]{2,1,0:T(8,128)(2,1)S(1)} %maximum_bitcast_fusion.refs_0_, ...), custom_call_target="tpu_custom_call" | custom-call | flops 3221225472 | bytes 7340032 | tf_op jit(solution)/shard_map/rotated_step/pallas_call | solution.py:510
  198.9 1.7 collective-permute-start.47
  200.6 2.7 %collective-permute-start.48 = (bf16[3,32,512]{2,1,0:T(8,128)(2,1)S(1)}, bf16[3,32,512]{2,1,0:T(8,128)(2,1)S(1)}, u32[]{:S(2)}, u32[]{:S(2)}) collective-permute-start(bf16[3,32,512]{2,1,0:T(8,128)(2,1)S(1)} %get-tuple-element.256), channel_id=1, source_target_pairs={{0,24},{1,25},{2,26},{3,27},{4,28},{5,29},{6,30},{7,31},{8,16},{9,... | collective-permute-start | bytes 294920 | tf_op jit(solution)/shard_map/ppermute | solution.py:555
  203.2 3.5 %rotated_step.3 = (bf16[3,16,512]{2,1,0:T(8,128)(2,1)S(1)}, bf16[3,16,512]{2,1,0:T(8,128)(2,1)S(1)}, bf16[3,16,512]{2,1,0:T(8,128)(2,1)S(1)}, bf16[3,16,512]{2,1,0:T(8,128)(2,1)S(1)}) custom-call(s32[1]{0:T(128)} %bitcast.27.refs_0_.me_ref.refs_9_, bf16[4,64,512]{2,1,0:T(8,128)(2,1)S(1)} %maximum_bitcast_fusion.2.refs_0_, ...), custom_call_target="tpu_custom_call" | custom-call | flops 1073741824 | bytes 3145728 | tf_op jit(solution)/shard_map/rotated_step/pallas_call | solution.py:510
  208.5 2.7 %collective-permute-start.45 = (bf16[3,16,512]{2,1,0:T(8,128)(2,1)S(1)}, bf16[3,16,512]{2,1,0:T(8,128)(2,1)S(1)}, u32[]{:S(2)}, u32[]{:S(2)}) collective-permute-start(bf16[3,16,512]{2,1,0:T(8,128)(2,1)S(1)} %get-tuple-element.276), channel_id=1, source_target_pairs={{0,24},{1,25},{2,26},{3,27},{4,28},{5,29},{6,30},{7,31},{8,16},{9,... | collective-permute-start | bytes 147464 | tf_op jit(solution)/shard_map/ppermute | solution.py:555
  212.7 2.2 %collective-permute-done.44.refs_2_ = bf16[3,16,512]{2,1,0:T(8,128)(2,1)S(1)} collective-permute-done((bf16[3,16,512]{2,1,0:T(8,128)(2,1)S(1)}, bf16[3,16,512]{2,1,0:T(8,128)(2,1)S(1)}, u32[]{:S(2)}, u32[]{:S(2)}) %collective-permute-start.44) | collective-permute-done | bytes 49184 | tf_op jit(solution)/shard_map/ppermute | solution.py:555
  (183 shorter events, 51.2 us)
Async XLA Ops:
  27.1 31.2 %collective-permute-start.10 = (bf16[4,80,512]{2,1,0:T(8,128)(2,1)S(1)}, bf16[4,80,512]{2,1,0:T(8,128)(2,1)S(1)}, u32[]{:S(2)}, u32[]{:S(2)}) collective-permute-start(bf16[4,80,512]{2,1,0:T(8,128)(2,1)S(1)} %maximum_bitcast_fusion.1), channel_id=1, source_target_pairs={{0,2},{1,3},{2,0},{3,1},{4,6},{5,7},{6,4},{7,5},{8,10},{9,11},{10,... | collective-permute-start | bytes 983048 | tf_op jit(solution)/shard_map/ppermute | solution.py:555
  28.4 29.9 %collective-permute-start.11 = (bf16[4,80,512]{2,1,0:T(8,128)(2,1)S(1)}, bf16[4,80,512]{2,1,0:T(8,128)(2,1)S(1)}, u32[]{:S(2)}, u32[]{:S(2)}) collective-permute-start(bf16[4,80,512]{2,1,0:T(8,128)(2,1)S(1)} %maximum_bitcast_fusion.1), channel_id=1, source_target_pairs={{0,4},{1,5},{2,6},{3,7},{4,0},{5,1},{6,2},{7,3},{8,12},{9,13},{10,... | collective-permute-start | bytes 983048 | tf_op jit(solution)/shard_map/ppermute | solution.py:555
  29.9 28.4 %collective-permute-start.12 = (bf16[4,80,512]{2,1,0:T(8,128)(2,1)S(1)}, bf16[4,80,512]{2,1,0:T(8,128)(2,1)S(1)}, u32[]{:S(2)}, u32[]{:S(2)}) collective-permute-start(bf16[4,80,512]{2,1,0:T(8,128)(2,1)S(1)} %maximum_bitcast_fusion.1), channel_id=1, source_target_pairs={{0,6},{1,7},{2,4},{3,5},{4,2},{5,3},{6,0},{7,1},{8,14},{9,15},{10,... | collective-permute-start | bytes 983048 | tf_op jit(solution)/shard_map/ppermute | solution.py:555
  30.7 27.6 %collective-permute-start.14 = (bf16[2,48,512]{2,1,0:T(8,128)(2,1)S(1)}, bf16[2,48,512]{2,1,0:T(8,128)(2,1)S(1)}, u32[]{:S(2)}, u32[]{:S(2)}) collective-permute-start(bf16[2,48,512]{2,1,0:T(8,128)(2,1)S(1)} %pad_maximum_fusion.7), channel_id=1, source_target_pairs={{0,16},{1,17},{2,18},{3,19},{4,20},{5,21},{6,22},{7,23},{8,24},{9,... | collective-permute-start | bytes 294920 | tf_op jit(solution)/shard_map/ppermute | solution.py:555
  32.3 26.0 %collective-permute-start.15 = (bf16[2,48,512]{2,1,0:T(8,128)(2,1)S(1)}, bf16[2,48,512]{2,1,0:T(8,128)(2,1)S(1)}, u32[]{:S(2)}, u32[]{:S(2)}) collective-permute-start(bf16[2,48,512]{2,1,0:T(8,128)(2,1)S(1)} %pad_maximum_fusion.8), channel_id=1, source_target_pairs={{0,24},{1,25},{2,26},{3,27},{4,28},{5,29},{6,30},{7,31},{8,16},{9,... | collective-permute-start | bytes 294920 | tf_op jit(solution)/shard_map/ppermute | solution.py:555
  58.7 40.9 %collective-permute-start.17 = (bf16[4,2,48,512]{3,2,1,0:T(8,128)(2,1)S(1)}, bf16[4,2,48,512]{3,2,1,0:T(8,128)(2,1)S(1)}, u32[]{:S(2)}, u32[]{:S(2)}) collective-permute-start(bf16[4,2,48,512]{3,2,1,0:T(8,128)(2,1)S(1)} %pad_maximum_fusion.3), channel_id=1, source_target_pairs={{0,2},{1,3},{2,0},{3,1},{4,6},{5,7},{6,4},{7,5},{8,10},{9,11},{10,... | collective-permute-start | bytes 1179656 | tf_op jit(solution)/shard_map/ppermute | solution.py:555
  60.0 39.7 %collective-permute-start.18 = (bf16[4,2,48,512]{3,2,1,0:T(8,128)(2,1)S(1)}, bf16[4,2,48,512]{3,2,1,0:T(8,128)(2,1)S(1)}, u32[]{:S(2)}, u32[]{:S(2)}) collective-permute-start(bf16[4,2,48,512]{3,2,1,0:T(8,128)(2,1)S(1)} %pad_maximum_fusion.3), channel_id=1, source_target_pairs={{0,4},{1,5},{2,6},{3,7},{4,0},{5,1},{6,2},{7,3},{8,12},{9,13},{10,... | collective-permute-start | bytes 1179656 | tf_op jit(solution)/shard_map/ppermute | solution.py:555
  61.5 38.1 %collective-permute-start.19 = (bf16[4,2,48,512]{3,2,1,0:T(8,128)(2,1)S(1)}, bf16[4,2,48,512]{3,2,1,0:T(8,128)(2,1)S(1)}, u32[]{:S(2)}, u32[]{:S(2)}) collective-permute-start(bf16[4,2,48,512]{3,2,1,0:T(8,128)(2,1)S(1)} %pad_maximum_fusion.3), channel_id=1, source_target_pairs={{0,6},{1,7},{2,4},{3,5},{4,2},{5,3},{6,0},{7,1},{8,14},{9,15},{10,... | collective-permute-start | bytes 1179656 | tf_op jit(solution)/shard_map/ppermute | solution.py:555
  99.9 36.8 %collective-permute-start.24 = (bf16[16,2,48,512]{3,2,1,0:T(8,128)(2,1)S(1)}, bf16[16,2,48,512]{3,2,1,0:T(8,128)(2,1)S(1)}, u32[]{:S(2)}, u32[]{:S(2)}) collective-permute-start(bf16[16,2,48,512]{3,2,1,0:T(8,128)(2,1)S(1)} %bitcast.122), channel_id=1, source_target_pairs={{0,1},{1,0},{2,3},{3,2},{4,5},{5,4},{6,7},{7,6},{8,9},{9,8},{10,11... | collective-permute-start | bytes 4718600 | tf_op jit(solution)/shard_map/ppermute | solution.py:555
  104.1 32.6 %collective-permute-start.21 = (bf16[1,336,512]{2,1,0:T(8,128)(2,1)}, bf16[1,336,512]{2,1,0:T(8,128)(2,1)S(1)}, u32[]{:S(2)}, u32[]{:S(2)}) collective-permute-start(bf16[1,336,512]{2,1,0:T(8,128)(2,1)} %get-tuple-element.202), channel_id=1, source_target_pairs={{0,2},{1,3},{2,0},{3,1},{4,6},{5,7},{6,4},{7,5},{8,10},{9,11},{10,... | collective-permute-start | bytes 1032200 | tf_op jit(solution)/shard_map/ppermute | solution.py:555
  105.3 31.4 %collective-permute-start.22 = (bf16[1,336,512]{2,1,0:T(8,128)(2,1)}, bf16[1,336,512]{2,1,0:T(8,128)(2,1)S(1)}, u32[]{:S(2)}, u32[]{:S(2)}) collective-permute-start(bf16[1,336,512]{2,1,0:T(8,128)(2,1)} %get-tuple-element.203), channel_id=1, source_target_pairs={{0,4},{1,5},{2,6},{3,7},{4,0},{5,1},{6,2},{7,3},{8,12},{9,13},{10,... | collective-permute-start | bytes 1032200 | tf_op jit(solution)/shard_map/ppermute | solution.py:555
  106.8 29.9 %collective-permute-start.23 = (bf16[1,336,512]{2,1,0:T(8,128)(2,1)}, bf16[1,336,512]{2,1,0:T(8,128)(2,1)S(1)}, u32[]{:S(2)}, u32[]{:S(2)}) collective-permute-start(bf16[1,336,512]{2,1,0:T(8,128)(2,1)} %get-tuple-element.204), channel_id=1, source_target_pairs={{0,6},{1,7},{2,4},{3,5},{4,2},{5,3},{6,0},{7,1},{8,14},{9,15},{10,... | collective-permute-start | bytes 1032200 | tf_op jit(solution)/shard_map/ppermute | solution.py:555
  138.1 22.7 %collective-permute-start.25 = (bf16[144,512]{1,0:T(8,128)(2,1)}, bf16[144,512]{1,0:T(8,128)(2,1)S(1)}, u32[]{:S(2)}, u32[]{:S(2)}) collective-permute-start(bf16[144,512]{1,0:T(8,128)(2,1)} %get-tuple-element.213), channel_id=1, source_target_pairs={{0,8},{1,9},{2,10},{3,11},{4,12},{5,13},{6,14},{7,15},{8,0},{9,1},... | collective-permute-start | bytes 442376 | tf_op jit(solution)/shard_map/ppermute | solution.py:555
  138.1 22.7 %collective-permute-start.26 = (bf16[144,512]{1,0:T(8,128)(2,1)}, bf16[144,512]{1,0:T(8,128)(2,1)S(1)}, u32[]{:S(2)}, u32[]{:S(2)}) collective-permute-start(bf16[144,512]{1,0:T(8,128)(2,1)} %get-tuple-element.214), channel_id=1, source_target_pairs={{0,16},{1,17},{2,18},{3,19},{4,20},{5,21},{6,22},{7,23},{8,24},{9,... | collective-permute-start | bytes 442376 | tf_op jit(solution)/shard_map/ppermute | solution.py:555
  139.8 21.0 %collective-permute-start.27 = (bf16[144,512]{1,0:T(8,128)(2,1)}, bf16[144,512]{1,0:T(8,128)(2,1)S(1)}, u32[]{:S(2)}, u32[]{:S(2)}) collective-permute-start(bf16[144,512]{1,0:T(8,128)(2,1)} %get-tuple-element.215), channel_id=1, source_target_pairs={{0,24},{1,25},{2,26},{3,27},{4,28},{5,29},{6,30},{7,31},{8,16},{9,... | collective-permute-start | bytes 442376 | tf_op jit(solution)/shard_map/ppermute | solution.py:555
  161.0 9.8 %collective-permute-start.30 = (bf16[1,128,512]{2,1,0:T(8,128)(2,1)S(1)}, bf16[1,128,512]{2,1,0:T(8,128)(2,1)S(1)}, u32[]{:S(2)}, u32[]{:S(2)}) collective-permute-start(bf16[1,128,512]{2,1,0:T(8,128)(2,1)S(1)} %bitcast.127), channel_id=1, source_target_pairs={{0,2},{1,3},{2,0},{3,1},{4,6},{5,7},{6,4},{7,5},{8,10},{9,11},{10,... | collective-permute-start | bytes 393224 | tf_op jit(solution)/shard_map/ppermute | solution.py:555
  162.2 10.7 %collective-permute-start.31 = (bf16[1,128,512]{2,1,0:T(8,128)(2,1)S(1)}, bf16[1,128,512]{2,1,0:T(8,128)(2,1)S(1)}, u32[]{:S(2)}, u32[]{:S(2)}) collective-permute-start(bf16[1,128,512]{2,1,0:T(8,128)(2,1)S(1)} %bitcast.128), channel_id=1, source_target_pairs={{0,4},{1,5},{2,6},{3,7},{4,0},{5,1},{6,2},{7,3},{8,12},{9,13},{10,... | collective-permute-start | bytes 393224 | tf_op jit(solution)/shard_map/ppermute | solution.py:555
  166.7 11.5 %collective-permute-start.33 = (bf16[1,3,64,512]{3,2,1,0:T(8,128)(2,1)}, bf16[1,3,64,512]{3,2,1,0:T(8,128)(2,1)S(1)}, u32[]{:S(2)}, u32[]{:S(2)}) collective-permute-start(bf16[1,3,64,512]{3,2,1,0:T(8,128)(2,1)} %get-tuple-element.232), channel_id=1, source_target_pairs={{0,4},{1,5},{2,6},{3,7},{4,0},{5,1},{6,2},{7,3},{8,12},{9,13},{10,... | collective-permute-start | bytes 589832 | tf_op jit(solution)/shard_map/ppermute | solution.py:555
  179.9 11.1 %collective-permute-start.35 = (bf16[64,512]{1,0:T(8,128)(2,1)}, bf16[64,512]{1,0:T(8,128)(2,1)S(1)}, u32[]{:S(2)}, u32[]{:S(2)}) collective-permute-start(bf16[64,512]{1,0:T(8,128)(2,1)} %get-tuple-element.246), channel_id=1, source_target_pairs={{0,8},{1,9},{2,10},{3,11},{4,12},{5,13},{6,14},{7,15},{8,0},{9,1},... | collective-permute-start | bytes 196616 | tf_op jit(solution)/shard_map/ppermute | solution.py:555
  179.9 11.1 %collective-permute-start.36 = (bf16[64,512]{1,0:T(8,128)(2,1)}, bf16[64,512]{1,0:T(8,128)(2,1)S(1)}, u32[]{:S(2)}, u32[]{:S(2)}) collective-permute-start(bf16[64,512]{1,0:T(8,128)(2,1)} %get-tuple-element.247), channel_id=1, source_target_pairs={{0,16},{1,17},{2,18},{3,19},{4,20},{5,21},{6,22},{7,23},{8,24},{9,... | collective-permute-start | bytes 196616 | tf_op jit(solution)/shard_map/ppermute | solution.py:555
  181.6 9.4 %collective-permute-start.37 = (bf16[64,512]{1,0:T(8,128)(2,1)}, bf16[64,512]{1,0:T(8,128)(2,1)S(1)}, u32[]{:S(2)}, u32[]{:S(2)}) collective-permute-start(bf16[64,512]{1,0:T(8,128)(2,1)} %get-tuple-element.248), channel_id=1, source_target_pairs={{0,24},{1,25},{2,26},{3,27},{4,28},{5,29},{6,30},{7,31},{8,16},{9,... | collective-permute-start | bytes 196616 | tf_op jit(solution)/shard_map/ppermute | solution.py:555
  198.8 9.8 %collective-permute-start.46 = (bf16[3,32,512]{2,1,0:T(8,128)(2,1)S(1)}, bf16[3,32,512]{2,1,0:T(8,128)(2,1)S(1)}, u32[]{:S(2)}, u32[]{:S(2)}) collective-permute-start(bf16[3,32,512]{2,1,0:T(8,128)(2,1)S(1)} %get-tuple-element.254), channel_id=1, source_target_pairs={{0,8},{1,9},{2,10},{3,11},{4,12},{5,13},{6,14},{7,15},{8,0},{9,1},... | collective-permute-start | bytes 294920 | tf_op jit(solution)/shard_map/ppermute | solution.py:555
  198.9 12.4 %collective-permute-start.47 = (bf16[3,32,512]{2,1,0:T(8,128)(2,1)S(1)}, bf16[3,32,512]{2,1,0:T(8,128)(2,1)S(1)}, u32[]{:S(2)}, u32[]{:S(2)}) collective-permute-start(bf16[3,32,512]{2,1,0:T(8,128)(2,1)S(1)} %get-tuple-element.255), channel_id=1, source_target_pairs={{0,16},{1,17},{2,18},{3,19},{4,20},{5,21},{6,22},{7,23},{8,24},{9,... | collective-permute-start | bytes 294920 | tf_op jit(solution)/shard_map/ppermute | solution.py:555
  200.6 10.7 %collective-permute-start.48 = (bf16[3,32,512]{2,1,0:T(8,128)(2,1)S(1)}, bf16[3,32,512]{2,1,0:T(8,128)(2,1)S(1)}, u32[]{:S(2)}, u32[]{:S(2)}) collective-permute-start(bf16[3,32,512]{2,1,0:T(8,128)(2,1)S(1)} %get-tuple-element.256), channel_id=1, source_target_pairs={{0,24},{1,25},{2,26},{3,27},{4,28},{5,29},{6,30},{7,31},{8,16},{9,... | collective-permute-start | bytes 294920 | tf_op jit(solution)/shard_map/ppermute | solution.py:555
  (47 other events, 420.3 us)

commit v2 on v1

--- a/solution.py
+++ b/solution.py
@@ -14,10 +14,10 @@
 SLOTS = 1128
 STEP = 10
 PAD = 1152
-RB = 384
+RB = 576
 NRB = PAD // RB
 RBL = 576
-SUB = 128
+SUB = 144
 NRBL = PAD // RBL
 scaling = HD ** (-0.5)
 eps_norm = 1e-05
@@ -29,10 +29,10 @@
 axes = ("dp", "fsdp")
 bf16 = jnp.bfloat16
 f32 = jnp.float32
-VLIM_FWD = 58 * 1024 * 1024
+VLIM_FWD = 52 * 1024 * 1024
 VLIM_ROWS = 46 * 1024 * 1024
 VLIM_BWD = 46 * 1024 * 1024
-VLIM_STEP = 24 * 1024 * 1024
+VLIM_STEP = 20 * 1024 * 1024
 
 
 def nt(a, b):

time: 217 us -> 217 us (level)
    pallas_call x2, Pallas kernels: 47.4 us -> 36.4 us  [attn_bwd(): pl.pallas_call(functools.partial(attn_bwd_body, bool(cut)), grid=(n, NRBL...]
    pallas_call x1, Pallas kernels: 37.4 us -> 48 us  [rows_pass(): pl.pallas_call(functools.partial(rows_body, len(rest)), grid_spec=pltpu.P...]
  transfers between devices with their start and end apart: 49 -> 49, of which waited for: 12 -> 12; matrix products, arithmetic and copies ran while one was open for 5% -> 5% of each run, Pallas kernels for 56% -> 55%
where the time goes in v2:
time: 217 us; the launch traced here: 216 us
  Pallas kernels  123 us (57%)
  starting transfers between devices  55.4 us (26%)
  waiting for transfers between devices  22.8 us (11%)
  local copies, waits for them, and re-layouts  7.06 us (3%)
  other arithmetic  5.55 us (3%)
    ppermute x49, starting transfers between devices, swap(): return lax.ppermute(value, axes, pairs)  55.4 us
    pallas_call x1, Pallas kernels, rows_pass(): pl.pallas_call(functools.partial(rows_body, len(rest)), grid_spec=pltpu.P...  48 us
    pallas_call x2, Pallas kernels, attn_bwd(): pl.pallas_call(functools.partial(attn_bwd_body, bool(cut)), grid=(n, NRBL...  36.4 us
    ppermute x49, waiting for transfers between devices, swap(): return lax.ppermute(value, axes, pairs)  22.8 us
    pallas_call x1, Pallas kernels, attn_fwd(): pl.pallas_call(functools.partial(attn_fwd_body, len(parts)), grid=(n, NRB...  22.7 us
    pallas_call x2, Pallas kernels, rotated_step_parts(): pl.pallas_call(rotate_parts_body, grid=(1,), in_specs=[pl.BlockSpec(memor...  10.3 us
  transfers between devices with their start and end apart: 49, of which 12 were waited for; matrix products, arithmetic and copies ran while one was open for 5% of the time, Pallas kernels for 55%

profile of v2, /device:TPU:0, one launch (start us, length us, event | category | flops | bytes accessed | tf_op | source)
XLA Modules:
  0.0 215.8 jit_solution(2938877752365108546)
XLA Ops:
  1.7 3.1 %collective-permute-start = (bf16[1,3,16,512]{3,2,1,0:T(8,128)(2,1)S(1)}, bf16[1,3,16,512]{3,2,1,0:T(8,128)(2,1)S(1)}, u32[]{:S(2)}, u32[]{:S(2)}) collective-permute-start(bf16[1,3,16,512]{3,2,1,0:T(8,128)(2,1)S(1)} %get-tuple-element.313), channel_id=1, source_target_pairs={{0,8},{1,9},{2,10},{3,11},{4,12},{5,13},{6,14},{7,15},{8,0},{9,1},... | collective-permute-start | bytes 147464 | tf_op jit(solution)/shard_map/ppermute | solution.py:555
  4.8 2.6 %collective-permute-start.1 = (bf16[1,3,16,512]{3,2,1,0:T(8,128)(2,1)S(1)}, bf16[1,3,16,512]{3,2,1,0:T(8,128)(2,1)S(1)}, u32[]{:S(2)}, u32[]{:S(2)}) collective-permute-start(bf16[1,3,16,512]{3,2,1,0:T(8,128)(2,1)S(1)} %get-tuple-element.313), channel_id=1, source_target_pairs={{0,16},{1,17},{2,18},{3,19},{4,20},{5,21},{6,22},{7,23},{8,24},{9,... | collective-permute-start | bytes 147464 | tf_op jit(solution)/shard_map/ppermute | solution.py:555
  10.7 2.6 %collective-permute-done.2 = bf16[1,3,16,512]{3,2,1,0:T(8,128)(2,1)S(1)} collective-permute-done((bf16[1,3,16,512]{3,2,1,0:T(8,128)(2,1)S(1)}, bf16[1,3,16,512]{3,2,1,0:T(8,128)(2,1)S(1)}, u32[]{:S(2)}, u32[]{:S(2)}) %collective-permute-start.2) | collective-permute-done | bytes 49184 | tf_op jit(solution)/shard_map/ppermute | solution.py:555
  18.3 2.5 %collective-permute-done.6 = bf16[4,3,16,512]{3,2,1,0:T(8,128)(2,1)S(1)} collective-permute-done((bf16[4,3,16,512]{3,2,1,0:T(8,128)(2,1)S(1)}, bf16[4,3,16,512]{3,2,1,0:T(8,128)(2,1)S(1)}, u32[]{:S(2)}, u32[]{:S(2)}) %collective-permute-start.6) | collective-permute-done | bytes 196640 | tf_op jit(solution)/shard_map/ppermute | solution.py:555
  21.7 2.4 %collective-permute-done.7 = bf16[4,3,16,512]{3,2,1,0:T(8,128)(2,1)S(1)} collective-permute-done((bf16[4,3,16,512]{3,2,1,0:T(8,128)(2,1)S(1)}, bf16[4,3,16,512]{3,2,1,0:T(8,128)(2,1)S(1)}, u32[]{:S(2)}, u32[]{:S(2)}) %collective-permute-start.7) | collective-permute-done | bytes 196640 | tf_op jit(solution)/shard_map/ppermute | solution.py:555
  24.3 2.7 %collective-permute-done.5 = bf16[1,80,512]{2,1,0:T(8,128)(2,1)S(1)} collective-permute-done((bf16[1,80,512]{2,1,0:T(8,128)(2,1)S(1)}, bf16[1,80,512]{2,1,0:T(8,128)(2,1)S(1)}, u32[]{:S(2)}, u32[]{:S(2)}) %collective-permute-start.5) | collective-permute-done | bytes 81952 | tf_op jit(solution)/shard_map/ppermute | solution.py:555
  32.3 2.7 %collective-permute-start.15 = (bf16[2,48,512]{2,1,0:T(8,128)(2,1)S(1)}, bf16[2,48,512]{2,1,0:T(8,128)(2,1)S(1)}, u32[]{:S(2)}, u32[]{:S(2)}) collective-permute-start(bf16[2,48,512]{2,1,0:T(8,128)(2,1)S(1)} %pad_maximum_fusion.8), channel_id=1, source_target_pairs={{0,24},{1,25},{2,26},{3,27},{4,28},{5,29},{6,30},{7,31},{8,16},{9,... | collective-permute-start | bytes 294920 | tf_op jit(solution)/shard_map/ppermute | solution.py:555
  35.0 22.7 %attention_forward.1 = (bf16[2,1152,512]{2,1,0:T(8,128)(2,1)}, bf16[2,1024,512]{2,1,0:T(8,128)(2,1)}, bf16[2,1024,512]{2,1,0:T(8,128)(2,1)}, bf16[2,4,1152,1024]...) custom-call(s32[1]{0:T(128)} %bitcast.27.refs_0_.me_ref.refs_9_, ...), custom_call_target="tpu_custom_call" | custom-call | flops 14000000000 | bytes 40000000 | tf_op jit(solution)/shard_map/attention_forward/pallas_call | solution.py:103
  61.6 48.0 %rows_forward_backward.1 = (bf16[2,1128,512]{2,1,0:T(8,128)(2,1)}, f32[2,1128,512]{2,1,0:T(8,128)}, bf16[2,1152,512]{2,1,0:T(8,128)(2,1)}, bf16[4,336,512]{2,1,0:T(8,128)(2,1)S(1)}, bf16[4,336,512]{2,1,0:T(8,128)(2,1)S(1)}) custom-call(s32[3]{0:T(128)S(1)} %pad_add_fusion.cnt_ref, bf16[2,1128,512]{2,1,0:T(8,128)(2,1)} %refs_0_.3, ...), custom_call_target="tpu_custom_call" | custom-call | flops 17999998976 | bytes 30000000 | tf_op jit(solution)/shard_map/rows_forward_backward/pallas_call | solution.py:295
  110.6 2.3 %collective-permute-done.20.refs_1_ = bf16[4,336,512]{2,1,0:T(8,128)(2,1)S(1)} collective-permute-done((bf16[4,336,512]{2,1,0:T(8,128)(2,1)S(1)}, bf16[4,336,512]{2,1,0:T(8,128)(2,1)S(1)}, u32[]{:S(2)}, u32[]{:S(2)}) %collective-permute-start.20) | collective-permute-done | bytes 1376288 | tf_op jit(solution)/shard_map/ppermute | solution.py:555
  117.7 18.1 %attention_backward.2 = (f32[2,1128,512]{2,1,0:T(8,128)}, f32[3,256,512]{2,1,0:T(8,128)S(1)}) custom-call(bf16[2,1128,512]{2,1,0:T(8,128)(2,1)} %refs_0_.3, bf16[2,1152,512]{2,1,0:T(8,128)(2,1)} %get-tuple-element.184.refs_1_, bf16[2,1024,512]{2,1,0:T(8,128)(2,1)S(1)} %copy-done, ...), custom_call_target="tpu_custom_call", output_to_operand_aliasing={{0}: (7, {})} | custom-call | flops 8999999488 | bytes 24000000 | tf_op jit(solution)/shard_map/attention_backward/pallas_call | solution.py:418
  137.1 1.7 collective-permute-start.26
  138.9 2.7 %collective-permute-start.27 = (bf16[144,512]{1,0:T(8,128)(2,1)}, bf16[144,512]{1,0:T(8,128)(2,1)S(1)}, u32[]{:S(2)}, u32[]{:S(2)}) collective-permute-start(bf16[144,512]{1,0:T(8,128)(2,1)} %get-tuple-element.215), channel_id=1, source_target_pairs={{0,24},{1,25},{2,26},{3,27},{4,28},{5,29},{6,30},{7,31},{8,16},{9,... | collective-permute-start | bytes 442376 | tf_op jit(solution)/shard_map/ppermute | solution.py:555
  141.5 18.3 %attention_backward.3 = (f32[2,1128,512]{2,1,0:T(8,128)}, bf16[4,3,64,512]{3,2,1,0:T(8,128)(2,1)S(1)}, bf16[4,3,64,512]{3,2,1,0:T(8,128)(2,1)S(1)}) custom-call(bf16[2,1128,512]{2,1,0:T(8,128)(2,1)} %refs_0_.3, bf16[2,1152,512]{2,1,0:T(8,128)(2,1)} %get-tuple-element.184.refs_1_, bf16[2,1024,512]{2,1,0:T(8,128)(2,1)S(1)} %copy-done, ...), custom_call_target="tpu_custom_call", output_to_operand_aliasing={{0}: (7, {})} | custom-call | flops 8999999488 | bytes 24000000 | tf_op jit(solution)/shard_map/attention_backward/pallas_call | solution.py:418
  167.3 2.5 %fusion.refs_2_ = bf16[1024,1024]{1,0:T(8,128)(2,1)S(1)} fusion(f32[2,1024,1024]{2,1,0:T(8,128)} %param.18, s32[]{:T(128)S(6)} %min.20), kind=kLoop, calls=%fused_computation.1 | loop fusion | bytes 4194308 | tf_op jit(solution)/shard_map/convert_element_type | solution.py:848
  173.6 3.8 %collective-permute-done.33.refs_2_ = bf16[1,3,64,512]{3,2,1,0:T(8,128)(2,1)S(1)} collective-permute-done((bf16[1,3,64,512]{3,2,1,0:T(8,128)(2,1)}, bf16[1,3,64,512]{3,2,1,0:T(8,128)(2,1)S(1)}, u32[]{:S(2)}, u32[]{:S(2)}) %collective-permute-start.33) | collective-permute-done | bytes 196640 | tf_op jit(solution)/shard_map/ppermute | solution.py:555
  179.1 1.7 collective-permute-start.36
  180.8 2.7 %collective-permute-start.37 = (bf16[64,512]{1,0:T(8,128)(2,1)}, bf16[64,512]{1,0:T(8,128)(2,1)S(1)}, u32[]{:S(2)}, u32[]{:S(2)}) collective-permute-start(bf16[64,512]{1,0:T(8,128)(2,1)} %get-tuple-element.248), channel_id=1, source_target_pairs={{0,24},{1,25},{2,26},{3,27},{4,28},{5,29},{6,30},{7,31},{8,16},{9,... | collective-permute-start | bytes 196616 | tf_op jit(solution)/shard_map/ppermute | solution.py:555
  183.4 6.7 %rotated_step.2 = (bf16[3,32,512]{2,1,0:T(8,128)(2,1)S(1)}, bf16[3,32,512]{2,1,0:T(8,128)(2,1)S(1)}, bf16[3,32,512]{2,1,0:T(8,128)(2,1)S(1)}, bf16[3,32,512]{2,1,0:T(8,128)(2,1)S(1)}) custom-call(s32[1]{0:T(128)} %bitcast.27.refs_0_.me_ref.refs_9_, bf16[4,128,512]{2,1,0:T(8,128)(2,1)S(1)} %maximum_bitcast_fusion.refs_0_, ...), custom_call_target="tpu_custom_call" | custom-call | flops 3221225472 | bytes 7340032 | tf_op jit(solution)/shard_map/rotated_step/pallas_call | solution.py:510
  199.7 2.7 %collective-permute-start.48 = (bf16[3,32,512]{2,1,0:T(8,128)(2,1)S(1)}, bf16[3,32,512]{2,1,0:T(8,128)(2,1)S(1)}, u32[]{:S(2)}, u32[]{:S(2)}) collective-permute-start(bf16[3,32,512]{2,1,0:T(8,128)(2,1)S(1)} %get-tuple-element.256), channel_id=1, source_target_pairs={{0,24},{1,25},{2,26},{3,27},{4,28},{5,29},{6,30},{7,31},{8,16},{9,... | collective-permute-start | bytes 294920 | tf_op jit(solution)/shard_map/ppermute | solution.py:555
  202.4 3.6 %rotated_step.3 = (bf16[3,16,512]{2,1,0:T(8,128)(2,1)S(1)}, bf16[3,16,512]{2,1,0:T(8,128)(2,1)S(1)}, bf16[3,16,512]{2,1,0:T(8,128)(2,1)S(1)}, bf16[3,16,512]{2,1,0:T(8,128)(2,1)S(1)}) custom-call(s32[1]{0:T(128)} %bitcast.27.refs_0_.me_ref.refs_9_, bf16[4,64,512]{2,1,0:T(8,128)(2,1)S(1)} %maximum_bitcast_fusion.2.refs_0_, ...), custom_call_target="tpu_custom_call" | custom-call | flops 1073741824 | bytes 3145728 | tf_op jit(solution)/shard_map/rotated_step/pallas_call | solution.py:510
  206.0 1.7 collective-permute-start.44
  207.7 2.7 %collective-permute-start.45 = (bf16[3,16,512]{2,1,0:T(8,128)(2,1)S(1)}, bf16[3,16,512]{2,1,0:T(8,128)(2,1)S(1)}, u32[]{:S(2)}, u32[]{:S(2)}) collective-permute-start(bf16[3,16,512]{2,1,0:T(8,128)(2,1)S(1)} %get-tuple-element.276), channel_id=1, source_target_pairs={{0,24},{1,25},{2,26},{3,27},{4,28},{5,29},{6,30},{7,31},{8,16},{9,... | collective-permute-start | bytes 147464 | tf_op jit(solution)/shard_map/ppermute | solution.py:555
  211.9 2.2 %collective-permute-done.44.refs_2_ = bf16[3,16,512]{2,1,0:T(8,128)(2,1)S(1)} collective-permute-done((bf16[3,16,512]{2,1,0:T(8,128)(2,1)S(1)}, bf16[3,16,512]{2,1,0:T(8,128)(2,1)S(1)}, u32[]{:S(2)}, u32[]{:S(2)}) %collective-permute-start.44) | collective-permute-done | bytes 49184 | tf_op jit(solution)/shard_map/ppermute | solution.py:555
  (179 shorter events, 51.2 us)
Async XLA Ops:
  27.1 30.6 %collective-permute-start.10 = (bf16[4,80,512]{2,1,0:T(8,128)(2,1)S(1)}, bf16[4,80,512]{2,1,0:T(8,128)(2,1)S(1)}, u32[]{:S(2)}, u32[]{:S(2)}) collective-permute-start(bf16[4,80,512]{2,1,0:T(8,128)(2,1)S(1)} %maximum_bitcast_fusion.1), channel_id=1, source_target_pairs={{0,2},{1,3},{2,0},{3,1},{4,6},{5,7},{6,4},{7,5},{8,10},{9,11},{10,... | collective-permute-start | bytes 983048 | tf_op jit(solution)/shard_map/ppermute | solution.py:555
  28.4 29.3 %collective-permute-start.11 = (bf16[4,80,512]{2,1,0:T(8,128)(2,1)S(1)}, bf16[4,80,512]{2,1,0:T(8,128)(2,1)S(1)}, u32[]{:S(2)}, u32[]{:S(2)}) collective-permute-start(bf16[4,80,512]{2,1,0:T(8,128)(2,1)S(1)} %maximum_bitcast_fusion.1), channel_id=1, source_target_pairs={{0,4},{1,5},{2,6},{3,7},{4,0},{5,1},{6,2},{7,3},{8,12},{9,13},{10,... | collective-permute-start | bytes 983048 | tf_op jit(solution)/shard_map/ppermute | solution.py:555
  29.9 27.8 %collective-permute-start.12 = (bf16[4,80,512]{2,1,0:T(8,128)(2,1)S(1)}, bf16[4,80,512]{2,1,0:T(8,128)(2,1)S(1)}, u32[]{:S(2)}, u32[]{:S(2)}) collective-permute-start(bf16[4,80,512]{2,1,0:T(8,128)(2,1)S(1)} %maximum_bitcast_fusion.1), channel_id=1, source_target_pairs={{0,6},{1,7},{2,4},{3,5},{4,2},{5,3},{6,0},{7,1},{8,14},{9,15},{10,... | collective-permute-start | bytes 983048 | tf_op jit(solution)/shard_map/ppermute | solution.py:555
  30.7 27.0 %collective-permute-start.14 = (bf16[2,48,512]{2,1,0:T(8,128)(2,1)S(1)}, bf16[2,48,512]{2,1,0:T(8,128)(2,1)S(1)}, u32[]{:S(2)}, u32[]{:S(2)}) collective-permute-start(bf16[2,48,512]{2,1,0:T(8,128)(2,1)S(1)} %pad_maximum_fusion.7), channel_id=1, source_target_pairs={{0,16},{1,17},{2,18},{3,19},{4,20},{5,21},{6,22},{7,23},{8,24},{9,... | collective-permute-start | bytes 294920 | tf_op jit(solution)/shard_map/ppermute | solution.py:555
  32.3 25.4 %collective-permute-start.15 = (bf16[2,48,512]{2,1,0:T(8,128)(2,1)S(1)}, bf16[2,48,512]{2,1,0:T(8,128)(2,1)S(1)}, u32[]{:S(2)}, u32[]{:S(2)}) collective-permute-start(bf16[2,48,512]{2,1,0:T(8,128)(2,1)S(1)} %pad_maximum_fusion.8), channel_id=1, source_target_pairs={{0,24},{1,25},{2,26},{3,27},{4,28},{5,29},{6,30},{7,31},{8,16},{9,... | collective-permute-start | bytes 294920 | tf_op jit(solution)/shard_map/ppermute | solution.py:555
  58.1 51.6 %collective-permute-start.17 = (bf16[4,2,48,512]{3,2,1,0:T(8,128)(2,1)S(1)}, bf16[4,2,48,512]{3,2,1,0:T(8,128)(2,1)S(1)}, u32[]{:S(2)}, u32[]{:S(2)}) collective-permute-start(bf16[4,2,48,512]{3,2,1,0:T(8,128)(2,1)S(1)} %pad_maximum_fusion.3), channel_id=1, source_target_pairs={{0,2},{1,3},{2,0},{3,1},{4,6},{5,7},{6,4},{7,5},{8,10},{9,11},{10,... | collective-permute-start | bytes 1179656 | tf_op jit(solution)/shard_map/ppermute | solution.py:555
  59.3 50.3 %collective-permute-start.18 = (bf16[4,2,48,512]{3,2,1,0:T(8,128)(2,1)S(1)}, bf16[4,2,48,512]{3,2,1,0:T(8,128)(2,1)S(1)}, u32[]{:S(2)}, u32[]{:S(2)}) collective-permute-start(bf16[4,2,48,512]{3,2,1,0:T(8,128)(2,1)S(1)} %pad_maximum_fusion.3), channel_id=1, source_target_pairs={{0,4},{1,5},{2,6},{3,7},{4,0},{5,1},{6,2},{7,3},{8,12},{9,13},{10,... | collective-permute-start | bytes 1179656 | tf_op jit(solution)/shard_map/ppermute | solution.py:555
  60.9 48.8 %collective-permute-start.19 = (bf16[4,2,48,512]{3,2,1,0:T(8,128)(2,1)S(1)}, bf16[4,2,48,512]{3,2,1,0:T(8,128)(2,1)S(1)}, u32[]{:S(2)}, u32[]{:S(2)}) collective-permute-start(bf16[4,2,48,512]{3,2,1,0:T(8,128)(2,1)S(1)} %pad_maximum_fusion.3), channel_id=1, source_target_pairs={{0,6},{1,7},{2,4},{3,5},{4,2},{5,3},{6,0},{7,1},{8,14},{9,15},{10,... | collective-permute-start | bytes 1179656 | tf_op jit(solution)/shard_map/ppermute | solution.py:555
  110.0 25.8 %collective-permute-start.24 = (bf16[16,2,48,512]{3,2,1,0:T(8,128)(2,1)S(1)}, bf16[16,2,48,512]{3,2,1,0:T(8,128)(2,1)S(1)}, u32[]{:S(2)}, u32[]{:S(2)}) collective-permute-start(bf16[16,2,48,512]{3,2,1,0:T(8,128)(2,1)S(1)} %bitcast.124), channel_id=1, source_target_pairs={{0,1},{1,0},{2,3},{3,2},{4,5},{5,4},{6,7},{7,6},{8,9},{9,8},{10,11... | collective-permute-start | bytes 4718600 | tf_op jit(solution)/shard_map/ppermute | solution.py:555
  114.2 21.6 %collective-permute-start.21 = (bf16[1,336,512]{2,1,0:T(8,128)(2,1)}, bf16[1,336,512]{2,1,0:T(8,128)(2,1)S(1)}, u32[]{:S(2)}, u32[]{:S(2)}) collective-permute-start(bf16[1,336,512]{2,1,0:T(8,128)(2,1)} %get-tuple-element.202), channel_id=1, source_target_pairs={{0,2},{1,3},{2,0},{3,1},{4,6},{5,7},{6,4},{7,5},{8,10},{9,11},{10,... | collective-permute-start | bytes 1032200 | tf_op jit(solution)/shard_map/ppermute | solution.py:555
  115.4 20.4 %collective-permute-start.22 = (bf16[1,336,512]{2,1,0:T(8,128)(2,1)}, bf16[1,336,512]{2,1,0:T(8,128)(2,1)S(1)}, u32[]{:S(2)}, u32[]{:S(2)}) collective-permute-start(bf16[1,336,512]{2,1,0:T(8,128)(2,1)} %get-tuple-element.203), channel_id=1, source_target_pairs={{0,4},{1,5},{2,6},{3,7},{4,0},{5,1},{6,2},{7,3},{8,12},{9,13},{10,... | collective-permute-start | bytes 1032200 | tf_op jit(solution)/shard_map/ppermute | solution.py:555
  116.9 18.9 %collective-permute-start.23 = (bf16[1,336,512]{2,1,0:T(8,128)(2,1)}, bf16[1,336,512]{2,1,0:T(8,128)(2,1)S(1)}, u32[]{:S(2)}, u32[]{:S(2)}) collective-permute-start(bf16[1,336,512]{2,1,0:T(8,128)(2,1)} %get-tuple-element.204), channel_id=1, source_target_pairs={{0,6},{1,7},{2,4},{3,5},{4,2},{5,3},{6,0},{7,1},{8,14},{9,15},{10,... | collective-permute-start | bytes 1032200 | tf_op jit(solution)/shard_map/ppermute | solution.py:555
  137.1 22.7 %collective-permute-start.25 = (bf16[144,512]{1,0:T(8,128)(2,1)}, bf16[144,512]{1,0:T(8,128)(2,1)S(1)}, u32[]{:S(2)}, u32[]{:S(2)}) collective-permute-start(bf16[144,512]{1,0:T(8,128)(2,1)} %get-tuple-element.213), channel_id=1, source_target_pairs={{0,8},{1,9},{2,10},{3,11},{4,12},{5,13},{6,14},{7,15},{8,0},{9,1},... | collective-permute-start | bytes 442376 | tf_op jit(solution)/shard_map/ppermute | solution.py:555
  137.1 22.7 %collective-permute-start.26 = (bf16[144,512]{1,0:T(8,128)(2,1)}, bf16[144,512]{1,0:T(8,128)(2,1)S(1)}, u32[]{:S(2)}, u32[]{:S(2)}) collective-permute-start(bf16[144,512]{1,0:T(8,128)(2,1)} %get-tuple-element.214), channel_id=1, source_target_pairs={{0,16},{1,17},{2,18},{3,19},{4,20},{5,21},{6,22},{7,23},{8,24},{9,... | collective-permute-start | bytes 442376 | tf_op jit(solution)/shard_map/ppermute | solution.py:555
  138.9 21.1 %collective-permute-start.27 = (bf16[144,512]{1,0:T(8,128)(2,1)}, bf16[144,512]{1,0:T(8,128)(2,1)S(1)}, u32[]{:S(2)}, u32[]{:S(2)}) collective-permute-start(bf16[144,512]{1,0:T(8,128)(2,1)} %get-tuple-element.215), channel_id=1, source_target_pairs={{0,24},{1,25},{2,26},{3,27},{4,28},{5,29},{6,30},{7,31},{8,16},{9,... | collective-permute-start | bytes 442376 | tf_op jit(solution)/shard_map/ppermute | solution.py:555
  160.1 9.8 %collective-permute-start.30 = (bf16[1,128,512]{2,1,0:T(8,128)(2,1)S(1)}, bf16[1,128,512]{2,1,0:T(8,128)(2,1)S(1)}, u32[]{:S(2)}, u32[]{:S(2)}) collective-permute-start(bf16[1,128,512]{2,1,0:T(8,128)(2,1)S(1)} %bitcast.129), channel_id=1, source_target_pairs={{0,2},{1,3},{2,0},{3,1},{4,6},{5,7},{6,4},{7,5},{8,10},{9,11},{10,... | collective-permute-start | bytes 393224 | tf_op jit(solution)/shard_map/ppermute | solution.py:555
  161.4 10.7 %collective-permute-start.31 = (bf16[1,128,512]{2,1,0:T(8,128)(2,1)S(1)}, bf16[1,128,512]{2,1,0:T(8,128)(2,1)S(1)}, u32[]{:S(2)}, u32[]{:S(2)}) collective-permute-start(bf16[1,128,512]{2,1,0:T(8,128)(2,1)S(1)} %bitcast.130), channel_id=1, source_target_pairs={{0,4},{1,5},{2,6},{3,7},{4,0},{5,1},{6,2},{7,3},{8,12},{9,13},{10,... | collective-permute-start | bytes 393224 | tf_op jit(solution)/shard_map/ppermute | solution.py:555
  165.8 11.6 %collective-permute-start.33 = (bf16[1,3,64,512]{3,2,1,0:T(8,128)(2,1)}, bf16[1,3,64,512]{3,2,1,0:T(8,128)(2,1)S(1)}, u32[]{:S(2)}, u32[]{:S(2)}) collective-permute-start(bf16[1,3,64,512]{3,2,1,0:T(8,128)(2,1)} %get-tuple-element.232), channel_id=1, source_target_pairs={{0,4},{1,5},{2,6},{3,7},{4,0},{5,1},{6,2},{7,3},{8,12},{9,13},{10,... | collective-permute-start | bytes 589832 | tf_op jit(solution)/shard_map/ppermute | solution.py:555
  179.0 11.1 %collective-permute-start.35 = (bf16[64,512]{1,0:T(8,128)(2,1)}, bf16[64,512]{1,0:T(8,128)(2,1)S(1)}, u32[]{:S(2)}, u32[]{:S(2)}) collective-permute-start(bf16[64,512]{1,0:T(8,128)(2,1)} %get-tuple-element.246), channel_id=1, source_target_pairs={{0,8},{1,9},{2,10},{3,11},{4,12},{5,13},{6,14},{7,15},{8,0},{9,1},... | collective-permute-start | bytes 196616 | tf_op jit(solution)/shard_map/ppermute | solution.py:555
  179.1 11.1 %collective-permute-start.36 = (bf16[64,512]{1,0:T(8,128)(2,1)}, bf16[64,512]{1,0:T(8,128)(2,1)S(1)}, u32[]{:S(2)}, u32[]{:S(2)}) collective-permute-start(bf16[64,512]{1,0:T(8,128)(2,1)} %get-tuple-element.247), channel_id=1, source_target_pairs={{0,16},{1,17},{2,18},{3,19},{4,20},{5,21},{6,22},{7,23},{8,24},{9,... | collective-permute-start | bytes 196616 | tf_op jit(solution)/shard_map/ppermute | solution.py:555
  180.8 9.4 %collective-permute-start.37 = (bf16[64,512]{1,0:T(8,128)(2,1)}, bf16[64,512]{1,0:T(8,128)(2,1)S(1)}, u32[]{:S(2)}, u32[]{:S(2)}) collective-permute-start(bf16[64,512]{1,0:T(8,128)(2,1)} %get-tuple-element.248), channel_id=1, source_target_pairs={{0,24},{1,25},{2,26},{3,27},{4,28},{5,29},{6,30},{7,31},{8,16},{9,... | collective-permute-start | bytes 196616 | tf_op jit(solution)/shard_map/ppermute | solution.py:555
  197.9 9.8 %collective-permute-start.46 = (bf16[3,32,512]{2,1,0:T(8,128)(2,1)S(1)}, bf16[3,32,512]{2,1,0:T(8,128)(2,1)S(1)}, u32[]{:S(2)}, u32[]{:S(2)}) collective-permute-start(bf16[3,32,512]{2,1,0:T(8,128)(2,1)S(1)} %get-tuple-element.254), channel_id=1, source_target_pairs={{0,8},{1,9},{2,10},{3,11},{4,12},{5,13},{6,14},{7,15},{8,0},{9,1},... | collective-permute-start | bytes 294920 | tf_op jit(solution)/shard_map/ppermute | solution.py:555
  198.0 12.4 %collective-permute-start.47 = (bf16[3,32,512]{2,1,0:T(8,128)(2,1)S(1)}, bf16[3,32,512]{2,1,0:T(8,128)(2,1)S(1)}, u32[]{:S(2)}, u32[]{:S(2)}) collective-permute-start(bf16[3,32,512]{2,1,0:T(8,128)(2,1)S(1)} %get-tuple-element.255), channel_id=1, source_target_pairs={{0,16},{1,17},{2,18},{3,19},{4,20},{5,21},{6,22},{7,23},{8,24},{9,... | collective-permute-start | bytes 294920 | tf_op jit(solution)/shard_map/ppermute | solution.py:555
  199.7 10.7 %collective-permute-start.48 = (bf16[3,32,512]{2,1,0:T(8,128)(2,1)S(1)}, bf16[3,32,512]{2,1,0:T(8,128)(2,1)S(1)}, u32[]{:S(2)}, u32[]{:S(2)}) collective-permute-start(bf16[3,32,512]{2,1,0:T(8,128)(2,1)S(1)} %get-tuple-element.256), channel_id=1, source_target_pairs={{0,24},{1,25},{2,26},{3,27},{4,28},{5,29},{6,30},{7,31},{8,16},{9,... | collective-permute-start | bytes 294920 | tf_op jit(solution)/shard_map/ppermute | solution.py:555
  (45 other events, 383.2 us)
